TPU v7x, 32 devices: a whole 2x2x4 slice. The times are simulated.
32 devices in a mesh: sec: 8 (over y, x, core), col: 4 (over z).
Axes of the slice: x: 2, y: 2, z: 4, core: 2. Of those that a mesh axis runs over, the one named last changes fastest.
Arguments:
- air_state: float32 [4, 64, 32768], P(None, None, ('sec', 'col')), may hold values from -6 to 6
- air_mix: float32 [64, 32768], P(None, ('sec', 'col')), may hold values from 0.1 to 4
- surface_forcing: float32 [4, 32768], P(None, ('sec', 'col')), may hold values from 0 to 2
- air_mask: int32 [32768], P(('sec', 'col')), may hold values 0 or 1
- ocean_sources: int32 [4, 32768], P(None, ('sec', 'col')), may hold values from 0 to 6143, as said below
- ocean_weights: float32 [4, 32768], P(None, ('sec', 'col')), may hold values from 0.1 to 0.5
- sea_state: float32 [2, 80, 16384], P(None, None, ('sec', 'col')), may hold values from -6 to 6
- sea_mix: float32 [80, 16384], P(None, ('sec', 'col')), may hold values from 0.1 to 4
- ice_cover: float32 [16384], P(('sec', 'col')), may hold values from 0.05 to 0.95
- sea_mask: int32 [16384], P(('sec', 'col')), may hold values 0 or 1
- air_sources: int32 [4, 16384], P(None, ('sec', 'col')), may hold values from 0 to 12287, as said below
- air_weights: float32 [4, 16384], P(None, ('sec', 'col')), may hold values from 0.1 to 0.5
Outputs:
- air_out: float32 [4, 64, 32768], P(None, None, ('sec', 'col'))
- sea_out: float32 [2, 80, 16384], P(None, None, ('sec', 'col'))
- ice_out: float32 [16384], P(('sec', 'col'))
Inputs may be any that keep to these rules, and one draw needn't show every extreme that they name: Section t holds ocean cells t * 2048 to (t + 1) * 2048 - 1 and atmosphere columns t * 4096 to (t + 1) * 4096 - 1. An entry s of ocean_sources names cell s mod 2048 of the section s // 2048 - 1 places after the column's own. An entry s of air_sources names column s mod 4096 of the section s // 4096 - 1 places after the cell's own.
All inputs are finite; a program needn't handle non-finite values. No bound on the sum of `air_mask` or of `sea_mask` on one device may be relied on, other than what follows from the above.
Results may differ from a plain program's by a relative error of at most 0.0001.
Values sent between devices are 32-bit elements; how exact they have to be, the bound alone decides.
No kernel may reach another device: no remote copies, remote signals or barrier semaphores. Data moves between devices by JAX's collectives and lax.ppermute only.
A program may use at most 64 MiB of HBM per device.

v0:
```python
import math

import jax
import jax.numpy as jnp
from jax import lax
from jax.experimental import pallas as pl
from jax.experimental.pallas import tpu as pltpu
from jax.sharding import PartitionSpec as P


STEPS = 2
LANES = 128
SUBS = 8
FLUXES = 5


def tile_rows(x):
    *lead, r, n = x.shape
    t = min(r, SUBS)
    y = x.reshape(*lead, r // t, t, n // LANES, LANES)
    return jnp.swapaxes(y, -3, -2).reshape(*lead, r * n // LANES, LANES)


def untile_rows(x, r, n):
    lead = x.shape[:-2]
    t = min(r, SUBS)
    y = x.reshape(*lead, r // t, n // LANES, t, LANES)
    return jnp.swapaxes(y, -3, -2).reshape(*lead, r, n)


def level_rows(level, tiles, height=SUBS):
    return pl.ds((level // height) * height * tiles + level % height, tiles, stride=height)


def split(x, size):
    if size & (size - 1) == 0:
        return x >> (size.bit_length() - 1), x & (size - 1)
    return x // size, x % size


def sec_partners():
    n = lax.axis_size("sec")
    if n % 2 == 0:
        return (
            [(i, i ^ 1) for i in range(n)],
            [(i, (i + 1) % n if i % 2 else (i - 1) % n) for i in range(n)],
        )
    return ([(i, (i + 1) % n) for i in range(n)], [(i, (i - 1) % n) for i in range(n)])


def section_slot(band, sec, n):
    odd = sec & 1 if n % 2 == 0 else 1
    return jnp.where(band == 1, 0, jnp.where((band == 0) == (odd == 1), 1, 2))


def col_pairs(j):
    n = lax.axis_size("col")
    if n & (n - 1) == 0:
        return [(i, i ^ j) for i in range(n)]
    return [(i, (i + j) % n) for i in range(n)]


def row_slot(owner, col, n):
    if n & (n - 1) == 0:
        return owner ^ col
    rest = col - owner
    return jnp.where(rest < 0, rest + n, rest)


def sec_exchange(x):
    return [lax.ppermute(x, "sec", pairs) for pairs in sec_partners()]


def col_exchange(pieces):
    got = [pieces[0]]
    for j in range(1, len(pieces)):
        got.append(lax.ppermute(pieces[j], "col", col_pairs(j)))
    return got


def factor(mix, depth, put):
    half = depth // 2
    one = jnp.ones_like(mix(0))
    sides = []
    for side in (0, 1):
        if side == 0:
            sides.append([one, one, None])
        else:
            sides.append([one + mix(depth - 1), one, None])
    scale = [None, None]
    last = [None, None]
    for step in range(half):
        for side in (0, 1):
            n, d, _ = sides[side]
            i = step if side == 0 else depth - 1 - step
            ahead = mix(i) if side == 0 else mix(i - 1)
            behind = None
            if step:
                behind = mix(i - 1) if side == 0 else mix(i)
            d1 = n + ahead * d
            r1 = 1.0 / d1
            inv = d * r1
            n1 = d1 + ahead * n
            if step % 4 == 3:
                d1, n1 = d1 * scale[side], n1 * scale[side]
            if step % 4 == 0:
                scale[side] = r1
            out = ahead * inv
            put(i, inv, out, None if behind is None else behind * inv)
            sides[side] = [n1, d1, None]
            last[side] = out
    return 1.0 / (1.0 - last[0] * last[1])


def apply_factor(rhs, depth, get, middle, keep, kept, store):
    half = depth // 2
    carry = [None, None]
    for step in range(half):
        for side in (0, 1):
            i = step if side == 0 else depth - 1 - step
            inv, _, back = get(i)
            r = rhs(i)
            value = None if r is None else r * inv
            if step and carry[side] is not None:
                moved = back * carry[side]
                value = moved if value is None else value + moved
            carry[side] = value
            if value is not None:
                keep(i, value)
    top, bottom = carry
    up, down = get(half - 1)[1], get(half)[1]
    x_top = (top if bottom is None else top + up * bottom) * middle
    x_bottom = down * x_top if bottom is None else bottom + down * x_top
    store(half - 1, x_top)
    store(half, x_bottom)
    xs = [x_top, x_bottom]
    for step in range(half - 2, -1, -1):
        for side in (0, 1):
            i = step if side == 0 else depth - 1 - step
            x = get(i)[1] * xs[side]
            if side == 0 or bottom is not None:
                x = x + kept(i)
            xs[side] = x
            store(i, x)


def fetch(pairs, sems):
    copies = [pltpu.make_async_copy(src, dst, sems.at[i]) for i, (src, dst) in enumerate(pairs)]
    for c in copies:
        c.start()
    return copies


def first_kernel(cols, secs, cells_here, cols_here,
                 sea_ref, ice_hbm, air_ref, src_hbm, w_hbm, forcing_hbm, mask_hbm, feed_hbm, feed_w_hbm, wet_hbm,
                 top_ref, code_ref, fixed_ref, feed_ref, ice_ref, wet_ref,
                 sea0, air0, src_ref, w_ref, forcing_ref, mask_ref, feed_in, feed_w, sems):
    tiles, sea_tiles = mask_ref.shape[0], ice_ref.shape[0]
    sec, col = lax.axis_index("sec"), lax.axis_index("col")
    copies = fetch(
        [(sea_ref.at[0, pl.ds(0, SUBS * sea_tiles)], sea0), (ice_hbm, ice_ref), (feed_hbm, feed_in), (feed_w_hbm, feed_w),
         (src_hbm, src_ref), (w_hbm, w_ref), (forcing_hbm, forcing_ref), (mask_hbm, mask_ref), (wet_hbm, wet_ref),
         (air_ref.at[:, pl.ds(0, SUBS * tiles)], air0)], sems)
    for c in copies:
        c.wait()
    top_ref[0:sea_tiles] = sea0[level_rows(0, sea_tiles), :]
    top_ref[sea_tiles:] = ice_ref[...]

    s = feed_in[...]
    band, within = split(s, cols_here * cols)
    owner, place = split(within, cols_here)
    code = (owner * 3 + section_slot(band, sec, secs)) * cols_here + place
    m = s.shape[0]
    feed_ref[0:m] = code.astype(jnp.float32)
    feed_ref[m : 2 * m] = feed_w[...]

    mask = mask_ref[...] == 1
    ks = src_ref.shape[0] // tiles
    for k in range(ks):
        s = src_ref[pl.ds(k, tiles, stride=ks), :]
        band, within = split(s, cells_here * cols)
        owner, place = split(within, cells_here)
        slot = section_slot(band, sec, secs) * cols + row_slot(owner, col, cols)
        code_ref[k] = slot * cells_here + place
        fixed_ref[k] = jnp.where(mask, w_ref[pl.ds(k, tiles, stride=ks), :], 0.0)
    nf = forcing_ref.shape[0] // tiles
    for k in range(nf):
        f = forcing_ref[pl.ds(k, tiles, stride=nf), :]
        fixed_ref[ks + k] = f if k < nf - 1 else jnp.where(mask, 0.0, f)
    for f in range(air0.shape[0]):
        fixed_ref[ks + nf + f] = air0[f, level_rows(0, tiles), :]


def air_prepare(air_hbm, mix_hbm, sea_hbm, sea_mix_hbm, y2_ref, hg_ref, top_ref, sea_ref, sea_mix_ref,
                air_ref, mix_ref, fac, work, x1, sems):
    depth = fac.shape[1]
    tiles = mix_ref.shape[0] // depth
    fields = air_ref.shape[0]
    copies = fetch(
        [(mix_hbm, mix_ref)] + [(air_hbm.at[f], air_ref.at[f]) for f in range(fields)]
        + [(sea_hbm, sea_ref), (sea_mix_hbm, sea_mix_ref)], sems)
    copies[0].wait()

    def put(i, inv, out, back):
        fac[0, i] = inv
        fac[1, i] = out
        if back is not None:
            fac[2, i] = back

    middle = factor(lambda i: mix_ref[level_rows(i, tiles), :], depth, put)

    class Get:
        def __call__(self, i):
            return (fac[0, i], fac[1, i], fac[2, i])

    get = Get()
    for f in [fields] + list(range(fields)):
        if f < fields:
            copies[1 + f].wait()

        def rhs(i, f=f):
            if f < fields:
                return air_ref[f, level_rows(i, tiles), :]
            return jnp.ones_like(middle) if i == 0 else None

        def keep(i, v, f=f):
            work[f, i] = v

        def kept(i, f=f):
            return work[f, i]

        def store(i, v, f=f):
            x1[f, i] = v
            if f == fields:
                hg_ref[1, level_rows(i, tiles), :] = v

        apply_factor(rhs, depth, get, middle, keep, kept, store)
        top_ref[f] = x1[f, 0]
    for f in range(fields + 1):
        def rhs(i, f=f):
            return x1[f, i]

        def keep(i, v, f=f):
            work[f, i] = v

        def kept(i, f=f):
            return work[f, i]

        def store(i, v, f=f):
            if f < fields:
                y2_ref[f, level_rows(i, tiles), :] = v
            else:
                hg_ref[0, level_rows(i, tiles), :] = v

        apply_factor(rhs, depth, get, middle, keep, kept, store)
    for c in copies[1 + fields :]:
        c.wait()


def first_bundle(own_ref, m1_ref, m2_ref, feed_ref, out_ref):
    n = own_ref.shape[0]
    later_bundle(own_ref, m1_ref, m2_ref, out_ref.at[0 : 3 * n])
    out_ref[3 * n :] = feed_ref[...]


def later_bundle(own_ref, m1_ref, m2_ref, out_ref):
    n = own_ref.shape[0]
    out_ref[0:n] = own_ref[...]
    out_ref[n : 2 * n] = m1_ref[...]
    out_ref[2 * n : 3 * n] = m2_ref[...]


def lane_gather(row, lane):
    return jnp.take_along_axis(jnp.broadcast_to(row, lane.shape), lane, axis=1)


def flux_kernel(later, pieces, cell_rows, *refs):
    tables, refs = refs[:pieces], refs[pieces:]
    code_ref, fixed_ref, refs = refs[0], refs[1], refs[2:]
    if later:
        top_ref, before_ref, refs = refs[0], refs[1], refs[2:]
    flux_ref, add_ref = refs
    ks = code_ref.shape[0]
    his, lanes, vals = [], [], []
    for k in range(ks):
        hi, lane = split(code_ref[k], LANES)
        his.append(hi)
        lanes.append(lane)
        vals.append([jnp.zeros(lane.shape, jnp.float32) for _ in range(2)])
    for slot in range(3):
        for j in range(pieces):
            for r in range(cell_rows):
                number = (slot * pieces + j) * cell_rows + r
                base = slot * 2 * cell_rows + r
                row0 = tables[j][base : base + 1, :]
                row1 = tables[j][base + cell_rows : base + cell_rows + 1, :]
                for k in range(ks):
                    hit = his[k] == number
                    vals[k][0] = jnp.where(hit, lane_gather(row0, lanes[k]), vals[k][0])
                    vals[k][1] = jnp.where(hit, lane_gather(row1, lanes[k]), vals[k][1])
    skin = fixed_ref[ks + 3]
    frozen = jnp.zeros_like(skin)
    for k in range(ks):
        skin = skin + fixed_ref[k] * vals[k][0]
        frozen = frozen + fixed_ref[k] * vals[k][1]
    bottom = [fixed_ref[ks + 4 + f] for f in range(4)]
    if later:
        g = top_ref[4]
        bottom = [top_ref[f] + g * before_ref[f] for f in range(4)]
    short, long_, rain = fixed_ref[ks], fixed_ref[ks + 1], fixed_ref[ks + 2]
    cover = 1.0 / (1.0 + frozen)
    speed = jnp.sqrt(bottom[2] * bottom[2] + bottom[3] * bottom[3] + 1.0)
    coefficient = 0.3 * speed * cover
    snow = 1.0 / (1.0 + jnp.exp(2.0 * skin))
    f0 = coefficient * (skin - bottom[0])
    f1 = coefficient * (0.5 * jnp.exp(0.3 * skin) - bottom[1])
    f2 = coefficient * bottom[2]
    f3 = coefficient * bottom[3]
    f4 = short * cover
    f5 = long_ - 0.2 * skin
    f6 = rain * (1.0 - snow)
    f7 = rain * snow
    n = skin.shape[0]
    for v, value in enumerate((f2, f3, f4 + f5 - f0 - f1, 0.4 * f1 - f6, f7)):
        flux_ref[v * n : (v + 1) * n] = value
    for v, value in enumerate((f0, f1, -f2, -f3)):
        add_ref[v] = value


def partial_kernel(pieces, offset, *refs):
    flux, refs = refs[:3], refs[3:]
    bundles, outs = refs[:pieces], refs[pieces:]
    col_rows = flux[0].shape[0] // FLUXES
    base = lax.axis_index("col") * (3 * col_rows)
    m = outs[0].shape[0] // FLUXES
    ks = (bundles[0].shape[0] - offset) // 2 // m
    per = SUBS // m
    for j in range(pieces):
        total = [None] * FLUXES
        for q in range(ks // per):
            code, w = [], []
            for k in range(q * per, (q + 1) * per):
                code.append(bundles[j][pl.ds(offset + k, m, stride=ks), :])
                w.append(bundles[j][pl.ds(offset + ks * m + k, m, stride=ks), :])
            code = jnp.concatenate(code, axis=0).astype(jnp.int32)
            w = jnp.concatenate(w, axis=0)
            hi, lane = split(code, LANES)
            hi = hi - base
            vals = [jnp.zeros(lane.shape, jnp.float32) for _ in range(FLUXES)]
            for slot in range(3):
                for r in range(col_rows):
                    hit = hi == slot * col_rows + r
                    for v in range(FLUXES):
                        row = flux[slot][v * col_rows + r : v * col_rows + r + 1, :]
                        vals[v] = jnp.where(hit, lane_gather(row, lane), vals[v])
            for v in range(FLUXES):
                part = w * vals[v]
                total[v] = part if total[v] is None else total[v] + part
        for v in range(FLUXES):
            whole = total[v][0:m]
            for p in range(1, per):
                whole = whole + total[v][p * m : (p + 1) * m]
            outs[j][v * m : (v + 1) * m] = whole


def sea_kernel(pieces, depth, last, *refs):
    parts, refs = refs[:pieces], refs[pieces:]
    state_ref, mix_ref, ice_ref, mask_ref, refs = refs[0], refs[1], refs[2], refs[3], refs[4:]
    out_ref, top_ref, fac, work = refs
    tiles = mix_ref.shape[0] // depth
    flux = []
    for v in range(FLUXES):
        total = parts[0][v * tiles : (v + 1) * tiles]
        for p in parts[1:]:
            total = total + p[v * tiles : (v + 1) * tiles]
        flux.append(total)
    ice = ice_ref[...]
    wet = mask_ref[...] == 1
    stress2 = 2.0 * jnp.sqrt(flux[0] * flux[0] + flux[1] * flux[1] + 0.01)
    heat, salt, snow = flux[2], flux[3], flux[4]
    open_water = 1.0 - ice
    adds = (0.5 * open_water * heat, 0.3 * open_water * salt)
    grown = ice / (ice + open_water * jnp.exp(0.5 * heat - 0.8 * snow))
    new_ice = jnp.where(wet, grown, ice)

    known = {}

    def mix(i):
        if i not in known:
            k = mix_ref[level_rows(i, tiles), :]
            known[i] = k * (1.0 + stress2 * math.exp(-i / 8.0))
        return known[i]

    def put(i, inv, out, back):
        fac[0, i] = inv
        fac[1, i] = out
        if back is not None:
            fac[2, i] = back

    middle = factor(mix, depth, put)
    for f in range(2):
        def rhs(i, f=f):
            r = state_ref[f, level_rows(i, tiles), :]
            return r + adds[f] if i == 0 else r

        def keep(i, v, f=f):
            work[f, i] = v

        def kept(i, f=f):
            return work[f, i]

        def store(i, v, f=f):
            new = jnp.where(wet, v, state_ref[f, level_rows(i, tiles), :])
            out_ref[f, level_rows(i, tiles), :] = new
            if f == 0 and i == 0 and not last:
                top_ref[0:tiles] = new

        apply_factor(rhs, depth, lambda i: (fac[0, i], fac[1, i], fac[2, i]), middle, keep, kept, store)
    if last:
        top_ref[...] = new_ice
    else:
        top_ref[tiles : 2 * tiles] = new_ice


def air_finish(y2_ref, hg_ref, first_ref, second_ref, out_ref):
    fields, tiles = first_ref.shape[0], first_ref.shape[1]
    rows = y2_ref.shape[1]
    for f in range(fields):
        for j in range(tiles):
            b1 = jnp.broadcast_to(first_ref[f, j : j + 1, :], (SUBS, LANES))
            b2 = jnp.broadcast_to(second_ref[f, j : j + 1, :], (SUBS, LANES))
            for t in range(rows // (SUBS * tiles)):
                at = slice((t * tiles + j) * SUBS, (t * tiles + j + 1) * SUBS)
                out_ref[f, at] = y2_ref[f, at] + hg_ref[0, at] * b1 + hg_ref[1, at] * b2


def call(kernel, out, *args, scratch=(), final=False, raw=False):
    many = isinstance(out, list)
    kind = jax.ShapeDtypeStruct if final else pltpu.VMEM
    return pl.pallas_call(
        kernel,
        out_shape=[kind(*o) for o in out] if many else kind(*out),
        in_specs=[pl.BlockSpec(memory_space=pltpu.HBM if raw else pltpu.VMEM)] * len(args),
        out_specs=[pl.BlockSpec(memory_space=pltpu.VMEM)] * len(out) if many else pl.BlockSpec(memory_space=pltpu.VMEM),
        scratch_shapes=list(scratch),
        compiler_params=pltpu.CompilerParams(vmem_limit_bytes=8 << 20),
    )(*[pltpu.with_memory_space_constraint(a, pltpu.HBM if raw else pltpu.VMEM) for a in args])


def per_device(air_state, air_mix, surface_forcing, air_mask, ocean_sources, ocean_weights,
               sea_state, sea_mix, ice_cover, sea_mask, air_sources, air_weights):
    cols, secs = lax.axis_size("col"), lax.axis_size("sec")
    fields, levels, here = air_state.shape
    depth, cells = sea_mix.shape
    tiles, sea_tiles = here // LANES, cells // LANES
    f32, i32 = jnp.float32, jnp.int32
    ko = ocean_sources.shape[0]

    air = tile_rows(air_state)
    mixing = tile_rows(air_mix)
    sea = tile_rows(sea_state)
    sea_k = tile_rows(sea_mix)
    ice = ice_cover.reshape(sea_tiles, LANES)
    wet = sea_mask.reshape(sea_tiles, LANES)

    offset = 6 * sea_tiles
    feed_rows = 2 * air_sources.shape[0] * sea_tiles
    smalls = [tile_rows(v) for v in (ocean_sources, ocean_weights, surface_forcing)]
    feeds = [tile_rows(v) for v in (air_sources, air_weights)]
    top, code, fixed, feed, ice, wet = call(
        lambda *r: first_kernel(cols, secs, cells, here, *r),
        [((2 * sea_tiles, LANES), f32), ((ko, tiles, LANES), i32), ((ko + 8, tiles, LANES), f32),
         ((feed_rows, LANES), f32), (ice.shape, f32), (wet.shape, i32)],
        sea, ice, air, *smalls, air_mask.reshape(tiles, LANES), *feeds, wet, raw=True,
        scratch=[pltpu.VMEM((SUBS * sea_tiles, LANES), f32), pltpu.VMEM((fields, SUBS * tiles, LANES), f32),
                 *[pltpu.VMEM(v.shape, v.dtype) for v in smalls], pltpu.VMEM((tiles, LANES), i32),
                 *[pltpu.VMEM(v.shape, v.dtype) for v in feeds], pltpu.SemaphoreType.DMA((10,))],
    )
    near = sec_exchange(top)
    bundle = call(first_bundle, ((offset + feed_rows, LANES), f32), top, *near, feed)
    y2, hg, tops, sea, sea_k = call(
        air_prepare,
        [(air.shape, f32), ((2,) + mixing.shape, f32), ((fields + 1, tiles, LANES), f32), (sea.shape, f32), (sea_k.shape, f32)],
        air, mixing, sea, sea_k, raw=True,
        scratch=[pltpu.VMEM(air.shape, f32), pltpu.VMEM(mixing.shape, f32), pltpu.VMEM((3, levels, tiles, LANES), f32),
                 pltpu.VMEM((fields + 1, levels, tiles, LANES), f32), pltpu.VMEM((fields + 1, levels, tiles, LANES), f32),
                 pltpu.SemaphoreType.DMA((fields + 3,))],
    )
    bundles = col_exchange([bundle] * cols)
    adds, tables = [], bundles
    for step in range(STEPS):
        extra = (tops, adds[0]) if step else ()
        flux, add = call(
            lambda *r: flux_kernel(bool(step), cols, sea_tiles, *r),
            [((FLUXES * tiles, LANES), f32), ((fields, tiles, LANES), f32)],
            *tables, code, fixed, *extra,
        )
        adds.append(add)
        parts = call(
            lambda *r: partial_kernel(cols, offset, *r),
            [((FLUXES * sea_tiles, LANES), f32)] * cols,
            flux, *sec_exchange(flux), *bundles,
        )
        moved = col_exchange(parts)
        last = step == STEPS - 1
        if last:
            air_out = call(air_finish, (air.shape, f32), y2, hg, *adds, final=True)
        sea, top = call(
            lambda *r: sea_kernel(cols, depth, last, *r),
            [(sea.shape, f32), ((sea_tiles if last else 2 * sea_tiles, LANES), f32)],
            *moved, sea, sea_k, ice, wet, final=last,
            scratch=[pltpu.VMEM((3, depth, sea_tiles, LANES), f32), pltpu.VMEM((2, depth, sea_tiles, LANES), f32)],
        )
        if not last:
            ice = top[sea_tiles:]
            bundle = call(later_bundle, ((offset, LANES), f32), top, *sec_exchange(top))
            tables = col_exchange([bundle] * cols)
    return (untile_rows(air_out, levels, here), untile_rows(sea, depth, cells), top.reshape(cells))


def solution(mesh):
    both = ("sec", "col")
    placed = (
        P(None, None, both), P(None, both), P(None, both), P(both), P(None, both), P(None, both),
        P(None, None, both), P(None, both), P(both), P(both), P(None, both), P(None, both),
    )
    return jax.shard_map(
        per_device,
        mesh=mesh,
        in_specs=placed,
        out_specs=(P(None, None, both), P(None, None, both), P(both)),
        check_vma=False,
    )
```

profile of v0, /device:TPU:0, one launch (start us, length us, event | category | flops | bytes accessed | tf_op | source)
XLA Modules:
  0.0 58.2 jit_solution(3486441887842131106)
XLA Ops:
  0.6 1.2 %shard_map.140 = (f32[8,128]{1,0:T(8,128)S(1)}, s32[4,8,128]{2,1,0:T(8,128)S(1)}, f32[12,8,128]{2,1,0:T(8,128)S(1)}, f32[32,128]{1,0:T(8,128)S(1)}, f32[4,128]{1,0:T(4,128)S(1)}, /*index=5*/s32[4,128]{1,0:T(4,128)S(1)}) custom-call(f32[2,320,128]{2,1,0:T(8,128)} %bitcast.61, f32[4,128]{1,0:T(4,128)} %bitcast.72, f32[4,512,128]{2,1,0:T(8,128)} %bitcast.59, ...), custom_call_target="tpu_custom_call" | custom-call | tf_op jit(solution)/shard_map/pallas_call | solution.py:440
  2.4 3.5 %collective-permute-start.1 = (f32[8,128]{1,0:T(8,128)S(1)}, f32[8,128]{1,0:T(8,128)S(1)}, u32[]{:S(2)}, u32[]{:S(2)}) collective-permute-start(f32[8,128]{1,0:T(8,128)S(1)} %get-tuple-element.32.own_ref), channel_id=1, source_target_pairs={{0,28},{4,8},{8,4},{12,16},{16,12},{20,24},{24,20},{28,0},{1,29},{... | collective-permute-start | bytes 12296 | tf_op jit(solution)/shard_map/ppermute | solution.py:71
  5.9 1.3 %collective-permute-done.1.m2_ref = f32[8,128]{1,0:T(8,128)S(1)} collective-permute-done((f32[8,128]{1,0:T(8,128)S(1)}, f32[8,128]{1,0:T(8,128)S(1)}, u32[]{:S(2)}, u32[]{:S(2)}) %collective-permute-start.1) | collective-permute-done | bytes 4128 | tf_op jit(solution)/shard_map/ppermute | solution.py:71
  7.2 1.7 %collective-permute-start.2 = (f32[56,128]{1,0:T(8,128)S(1)}, f32[56,128]{1,0:T(8,128)S(1)}, u32[]{:S(2)}, u32[]{:S(2)}) collective-permute-start(f32[56,128]{1,0:T(8,128)S(1)} %shard_map.141.r_0_.r_3_), channel_id=1, source_target_pairs={{0,1},{1,0},{2,3},{3,2},{4,5},{5,4},{6,7},{7,6},{8,9},{9,8},{10,11... | collective-permute-start | bytes 86024 | tf_op jit(solution)/shard_map/ppermute | solution.py:77
  8.9 2.6 %collective-permute-start.3 = (f32[56,128]{1,0:T(8,128)S(1)}, f32[56,128]{1,0:T(8,128)S(1)}, u32[]{:S(2)}, u32[]{:S(2)}) collective-permute-start(f32[56,128]{1,0:T(8,128)S(1)} %shard_map.141.r_0_.r_3_), channel_id=1, source_target_pairs={{0,2},{1,3},{2,0},{3,1},{4,6},{5,7},{6,4},{7,5},{8,10},{9,11},{10,... | collective-permute-start | bytes 86024 | tf_op jit(solution)/shard_map/ppermute | solution.py:77
  11.6 2.5 %collective-permute-done.3.r_2_.r_5_ = f32[56,128]{1,0:T(8,128)S(1)} collective-permute-done((f32[56,128]{1,0:T(8,128)S(1)}, f32[56,128]{1,0:T(8,128)S(1)}, u32[]{:S(2)}, u32[]{:S(2)}) %collective-permute-start.3) | collective-permute-done | bytes 28704 | tf_op jit(solution)/shard_map/ppermute | solution.py:77
  14.2 3.0 %collective-permute-done.4.r_3_.r_6_ = f32[56,128]{1,0:T(8,128)S(1)} collective-permute-done((f32[56,128]{1,0:T(8,128)S(1)}, f32[56,128]{1,0:T(8,128)S(1)}, u32[]{:S(2)}, u32[]{:S(2)}) %collective-permute-start.4) | collective-permute-done | bytes 28704 | tf_op jit(solution)/shard_map/ppermute | solution.py:77
  17.2 1.0 %shard_map.142 = (f32[40,128]{1,0:T(8,128)S(1)}, f32[4,8,128]{2,1,0:T(8,128)S(1)}) custom-call(f32[56,128]{1,0:T(8,128)S(1)} %shard_map.141.r_0_.r_3_, f32[56,128]{1,0:T(8,128)S(1)} %collective-permute-done.2.r_1_.r_4_, f32[56,128]{1,0:T(8,128)S(1)} %collective-permute-done.3.r_2_.r_5_, f32[56,128]{1,0:T(8,128)S(1)} %collective-permute-done.4.r_3_.r_6_, ...), custom_call_target="tpu_custom_call" | custom-call | tf_op jit(solution)/shard_map/pallas_call | solution.py:440
  18.3 1.8 %collective-permute-start.6 = (f32[40,128]{1,0:T(8,128)S(1)}, f32[40,128]{1,0:T(8,128)S(1)}, u32[]{:S(2)}, u32[]{:S(2)}) collective-permute-start(f32[40,128]{1,0:T(8,128)S(1)} %get-tuple-element.37.r_0_), channel_id=1, source_target_pairs={{0,28},{4,8},{8,4},{12,16},{16,12},{20,24},{24,20},{28,0},{1,29},{... | collective-permute-start | bytes 61448 | tf_op jit(solution)/shard_map/ppermute | solution.py:71
  20.0 2.4 %collective-permute-done.6.r_2_ = f32[40,128]{1,0:T(8,128)S(1)} collective-permute-done((f32[40,128]{1,0:T(8,128)S(1)}, f32[40,128]{1,0:T(8,128)S(1)}, u32[]{:S(2)}, u32[]{:S(2)}) %collective-permute-start.6) | collective-permute-done | bytes 20512 | tf_op jit(solution)/shard_map/ppermute | solution.py:71
  22.5 1.1 %shard_map.143 = (f32[20,128]{1,0:T(8,128)S(1)}, f32[20,128]{1,0:T(8,128)S(1)}, f32[20,128]{1,0:T(8,128)S(1)}, f32[20,128]{1,0:T(8,128)S(1)}) custom-call(f32[40,128]{1,0:T(8,128)S(1)} %get-tuple-element.37.r_0_, f32[40,128]{1,0:T(8,128)S(1)} %collective-permute-done.5.r_1_, f32[40,128]{1,0:T(8,128)S(1)} %collective-permute-done.6.r_2_, ...), custom_call_target="tpu_custom_call" | custom-call | tf_op jit(solution)/shard_map/pallas_call | solution.py:440
  24.5 3.5 %collective-permute-start.9 = (f32[20,128]{1,0:T(8,128)S(1)}, f32[20,128]{1,0:T(8,128)S(1)}, u32[]{:S(2)}, u32[]{:S(2)}) collective-permute-start(f32[20,128]{1,0:T(8,128)S(1)} %get-tuple-element.41), channel_id=1, source_target_pairs={{0,3},{1,2},{2,1},{3,0},{4,7},{5,6},{6,5},{7,4},{8,11},{9,10},{10,... | collective-permute-start | bytes 30728 | tf_op jit(solution)/shard_map/ppermute | solution.py:77
  28.1 2.1 %shard_map.139 = (f32[4,512,128]{2,1,0:T(8,128)S(1)}, f32[2,512,128]{2,1,0:T(8,128)S(1)}, f32[5,8,128]{2,1,0:T(8,128)S(1)}, f32[2,320,128]{2,1,0:T(8,128)S(1)}, f32[320,128]{1,0:T(8,128)S(1)}) custom-call(f32[4,512,128]{2,1,0:T(8,128)} %bitcast.60, f32[512,128]{1,0:T(8,128)} %bitcast.64, f32[2,320,128]{2,1,0:T(8,128)} %bitcast.62, f32[320,128]{1,0:T(8,128)} %bitcast.65), custom_call_target="tpu_custom_call" | custom-call | tf_op jit(solution)/shard_map/pallas_call | solution.py:440
  30.7 1.2 %collective-permute-start.11 = (f32[8,128]{1,0:T(8,128)S(1)}, f32[8,128]{1,0:T(8,128)S(1)}, u32[]{:S(2)}, u32[]{:S(2)}) collective-permute-start(f32[8,128]{1,0:T(8,128)S(1)} %get-tuple-element.46.own_ref), channel_id=1, source_target_pairs={{0,28},{4,8},{8,4},{12,16},{16,12},{20,24},{24,20},{28,0},{1,29},{... | collective-permute-start | bytes 12296 | tf_op jit(solution)/shard_map/ppermute | solution.py:71
  31.9 2.8 %collective-permute-done.11.m2_ref = f32[8,128]{1,0:T(8,128)S(1)} collective-permute-done((f32[8,128]{1,0:T(8,128)S(1)}, f32[8,128]{1,0:T(8,128)S(1)}, u32[]{:S(2)}, u32[]{:S(2)}) %collective-permute-start.11) | collective-permute-done | bytes 4128 | tf_op jit(solution)/shard_map/ppermute | solution.py:71
  34.8 3.8 %collective-permute-start.13 = (f32[24,128]{1,0:T(8,128)S(1)}, f32[24,128]{1,0:T(8,128)S(1)}, u32[]{:S(2)}, u32[]{:S(2)}) collective-permute-start(f32[24,128]{1,0:T(8,128)S(1)} %shard_map.145.r_0_), channel_id=1, source_target_pairs={{0,2},{1,3},{2,0},{3,1},{4,6},{5,7},{6,4},{7,5},{8,10},{9,11},{10,... | collective-permute-start | bytes 36872 | tf_op jit(solution)/shard_map/ppermute | solution.py:77
  39.1 1.3 %collective-permute-done.13.r_2_ = f32[24,128]{1,0:T(8,128)S(1)} collective-permute-done((f32[24,128]{1,0:T(8,128)S(1)}, f32[24,128]{1,0:T(8,128)S(1)}, u32[]{:S(2)}, u32[]{:S(2)}) %collective-permute-start.13) | collective-permute-done | bytes 12320 | tf_op jit(solution)/shard_map/ppermute | solution.py:77
  40.4 3.7 %collective-permute-done.14.r_3_ = f32[24,128]{1,0:T(8,128)S(1)} collective-permute-done((f32[24,128]{1,0:T(8,128)S(1)}, f32[24,128]{1,0:T(8,128)S(1)}, u32[]{:S(2)}, u32[]{:S(2)}) %collective-permute-start.14) | collective-permute-done | bytes 12320 | tf_op jit(solution)/shard_map/ppermute | solution.py:77
  44.1 1.0 %shard_map.146 = (f32[40,128]{1,0:T(8,128)S(1)}, f32[4,8,128]{2,1,0:T(8,128)S(1)}) custom-call(f32[24,128]{1,0:T(8,128)S(1)} %shard_map.145.r_0_, f32[24,128]{1,0:T(8,128)S(1)} %collective-permute-done.12.r_1_, f32[24,128]{1,0:T(8,128)S(1)} %collective-permute-done.13.r_2_, f32[24,128]{1,0:T(8,128)S(1)} %collective-permute-done.14.r_3_, ...), custom_call_target="tpu_custom_call" | custom-call | tf_op jit(solution)/shard_map/pallas_call | solution.py:440
  46.4 3.0 %collective-permute-done.16.r_2_ = f32[40,128]{1,0:T(8,128)S(1)} collective-permute-done((f32[40,128]{1,0:T(8,128)S(1)}, f32[40,128]{1,0:T(8,128)S(1)}, u32[]{:S(2)}, u32[]{:S(2)}) %collective-permute-start.16) | collective-permute-done | bytes 20512 | tf_op jit(solution)/shard_map/ppermute | solution.py:71
  49.4 1.1 %shard_map.148 = (f32[20,128]{1,0:T(8,128)S(1)}, f32[20,128]{1,0:T(8,128)S(1)}, f32[20,128]{1,0:T(8,128)S(1)}, f32[20,128]{1,0:T(8,128)S(1)}) custom-call(f32[40,128]{1,0:T(8,128)S(1)} %get-tuple-element.49.r_0_, f32[40,128]{1,0:T(8,128)S(1)} %collective-permute-done.15.r_1_, f32[40,128]{1,0:T(8,128)S(1)} %collective-permute-done.16.r_2_, ...), custom_call_target="tpu_custom_call" | custom-call | tf_op jit(solution)/shard_map/pallas_call | solution.py:440
  51.6 3.4 %collective-permute-start.19 = (f32[20,128]{1,0:T(8,128)S(1)}, f32[20,128]{1,0:T(8,128)S(1)}, u32[]{:S(2)}, u32[]{:S(2)}) collective-permute-start(f32[20,128]{1,0:T(8,128)S(1)} %get-tuple-element.53), channel_id=1, source_target_pairs={{0,3},{1,2},{2,1},{3,0},{4,7},{5,6},{6,5},{7,4},{8,11},{9,10},{10,... | collective-permute-start | bytes 30728 | tf_op jit(solution)/shard_map/ppermute | solution.py:77
  55.0 1.2 %shard_map.147 = f32[4,512,128]{2,1,0:T(8,128)} custom-call(f32[4,512,128]{2,1,0:T(8,128)S(1)} %get-tuple-element.30.y2_ref, f32[2,512,128]{2,1,0:T(8,128)S(1)} %get-tuple-element.31.hg_ref, f32[4,8,128]{2,1,0:T(8,128)S(1)} %get-tuple-element.36.r_7_.first_ref, f32[4,8,128]{2,1,0:T(8,128)S(1)} %get-tuple-element.48.second_ref), custom_call_target="tpu_custom_call" | custom-call | tf_op jit(solution)/shard_map/pallas_call | solution.py:440
  57.1 1.1 %shard_map.149 = (f32[2,320,128]{2,1,0:T(8,128)}, f32[4,128]{1,0:T(4,128)}) custom-call(f32[20,128]{1,0:T(8,128)S(1)} %get-tuple-element.50.r_0_, f32[20,128]{1,0:T(8,128)S(1)} %collective-permute-done.17.r_1_, f32[20,128]{1,0:T(8,128)S(1)} %collective-permute-done.18.r_2_, f32[20,128]{1,0:T(8,128)S(1)} %collective-permute-done.19.r_3_, ...), custom_call_target="tpu_custom_call" | custom-call | tf_op jit(solution)/shard_map/pallas_call | solution.py:440
  (28 shorter events, 6.0 us)
Async XLA Ops:
  1.8 4.1 %collective-permute-start = (f32[8,128]{1,0:T(8,128)S(1)}, f32[8,128]{1,0:T(8,128)S(1)}, u32[]{:S(2)}, u32[]{:S(2)}) collective-permute-start(f32[8,128]{1,0:T(8,128)S(1)} %get-tuple-element.32.own_ref), channel_id=1, source_target_pairs={{0,4},{4,0},{8,12},{12,8},{16,20},{20,16},{24,28},{28,24},{1,5},{5... | collective-permute-start | bytes 12296 | tf_op jit(solution)/shard_map/ppermute | solution.py:71
  2.4 4.9 %collective-permute-start.1 = (f32[8,128]{1,0:T(8,128)S(1)}, f32[8,128]{1,0:T(8,128)S(1)}, u32[]{:S(2)}, u32[]{:S(2)}) collective-permute-start(f32[8,128]{1,0:T(8,128)S(1)} %get-tuple-element.32.own_ref), channel_id=1, source_target_pairs={{0,28},{4,8},{8,4},{12,16},{16,12},{20,24},{24,20},{28,0},{1,29},{... | collective-permute-start | bytes 12296 | tf_op jit(solution)/shard_map/ppermute | solution.py:71
  7.2 4.4 %collective-permute-start.2 = (f32[56,128]{1,0:T(8,128)S(1)}, f32[56,128]{1,0:T(8,128)S(1)}, u32[]{:S(2)}, u32[]{:S(2)}) collective-permute-start(f32[56,128]{1,0:T(8,128)S(1)} %shard_map.141.r_0_.r_3_), channel_id=1, source_target_pairs={{0,1},{1,0},{2,3},{3,2},{4,5},{5,4},{6,7},{7,6},{8,9},{9,8},{10,11... | collective-permute-start | bytes 86024 | tf_op jit(solution)/shard_map/ppermute | solution.py:77
  8.9 5.2 %collective-permute-start.3 = (f32[56,128]{1,0:T(8,128)S(1)}, f32[56,128]{1,0:T(8,128)S(1)}, u32[]{:S(2)}, u32[]{:S(2)}) collective-permute-start(f32[56,128]{1,0:T(8,128)S(1)} %shard_map.141.r_0_.r_3_), channel_id=1, source_target_pairs={{0,2},{1,3},{2,0},{3,1},{4,6},{5,7},{6,4},{7,5},{8,10},{9,11},{10,... | collective-permute-start | bytes 86024 | tf_op jit(solution)/shard_map/ppermute | solution.py:77
  11.5 5.7 %collective-permute-start.4 = (f32[56,128]{1,0:T(8,128)S(1)}, f32[56,128]{1,0:T(8,128)S(1)}, u32[]{:S(2)}, u32[]{:S(2)}) collective-permute-start(f32[56,128]{1,0:T(8,128)S(1)} %shard_map.141.r_0_.r_3_), channel_id=1, source_target_pairs={{0,3},{1,2},{2,1},{3,0},{4,7},{5,6},{6,5},{7,4},{8,11},{9,10},{10,... | collective-permute-start | bytes 86024 | tf_op jit(solution)/shard_map/ppermute | solution.py:77
  18.2 1.8 %collective-permute-start.5 = (f32[40,128]{1,0:T(8,128)S(1)}, f32[40,128]{1,0:T(8,128)S(1)}, u32[]{:S(2)}, u32[]{:S(2)}) collective-permute-start(f32[40,128]{1,0:T(8,128)S(1)} %get-tuple-element.37.r_0_), channel_id=1, source_target_pairs={{0,4},{4,0},{8,12},{12,8},{16,20},{20,16},{24,28},{28,24},{1,5},{5... | collective-permute-start | bytes 61448 | tf_op jit(solution)/shard_map/ppermute | solution.py:71
  18.3 4.2 %collective-permute-start.6 = (f32[40,128]{1,0:T(8,128)S(1)}, f32[40,128]{1,0:T(8,128)S(1)}, u32[]{:S(2)}, u32[]{:S(2)}) collective-permute-start(f32[40,128]{1,0:T(8,128)S(1)} %get-tuple-element.37.r_0_), channel_id=1, source_target_pairs={{0,28},{4,8},{8,4},{12,16},{16,12},{20,24},{24,20},{28,0},{1,29},{... | collective-permute-start | bytes 61448 | tf_op jit(solution)/shard_map/ppermute | solution.py:71
  23.6 6.5 %collective-permute-start.7 = (f32[20,128]{1,0:T(8,128)S(1)}, f32[20,128]{1,0:T(8,128)S(1)}, u32[]{:S(2)}, u32[]{:S(2)}) collective-permute-start(f32[20,128]{1,0:T(8,128)S(1)} %get-tuple-element.39), channel_id=1, source_target_pairs={{0,1},{1,0},{2,3},{3,2},{4,5},{5,4},{6,7},{7,6},{8,9},{9,8},{10,11... | collective-permute-start | bytes 30728 | tf_op jit(solution)/shard_map/ppermute | solution.py:77
  23.7 6.5 %collective-permute-start.8 = (f32[20,128]{1,0:T(8,128)S(1)}, f32[20,128]{1,0:T(8,128)S(1)}, u32[]{:S(2)}, u32[]{:S(2)}) collective-permute-start(f32[20,128]{1,0:T(8,128)S(1)} %get-tuple-element.40), channel_id=1, source_target_pairs={{0,2},{1,3},{2,0},{3,1},{4,6},{5,7},{6,4},{7,5},{8,10},{9,11},{10,... | collective-permute-start | bytes 30728 | tf_op jit(solution)/shard_map/ppermute | solution.py:77
  24.5 5.6 %collective-permute-start.9 = (f32[20,128]{1,0:T(8,128)S(1)}, f32[20,128]{1,0:T(8,128)S(1)}, u32[]{:S(2)}, u32[]{:S(2)}) collective-permute-start(f32[20,128]{1,0:T(8,128)S(1)} %get-tuple-element.41), channel_id=1, source_target_pairs={{0,3},{1,2},{2,1},{3,0},{4,7},{5,6},{6,5},{7,4},{8,11},{9,10},{10,... | collective-permute-start | bytes 30728 | tf_op jit(solution)/shard_map/ppermute | solution.py:77
  30.6 1.3 %collective-permute-start.10 = (f32[8,128]{1,0:T(8,128)S(1)}, f32[8,128]{1,0:T(8,128)S(1)}, u32[]{:S(2)}, u32[]{:S(2)}) collective-permute-start(f32[8,128]{1,0:T(8,128)S(1)} %get-tuple-element.46.own_ref), channel_id=1, source_target_pairs={{0,4},{4,0},{8,12},{12,8},{16,20},{20,16},{24,28},{28,24},{1,5},{5... | collective-permute-start | bytes 12296 | tf_op jit(solution)/shard_map/ppermute | solution.py:71
  30.7 4.0 %collective-permute-start.11 = (f32[8,128]{1,0:T(8,128)S(1)}, f32[8,128]{1,0:T(8,128)S(1)}, u32[]{:S(2)}, u32[]{:S(2)}) collective-permute-start(f32[8,128]{1,0:T(8,128)S(1)} %get-tuple-element.46.own_ref), channel_id=1, source_target_pairs={{0,28},{4,8},{8,4},{12,16},{16,12},{20,24},{24,20},{28,0},{1,29},{... | collective-permute-start | bytes 12296 | tf_op jit(solution)/shard_map/ppermute | solution.py:71
  34.7 4.4 %collective-permute-start.12 = (f32[24,128]{1,0:T(8,128)S(1)}, f32[24,128]{1,0:T(8,128)S(1)}, u32[]{:S(2)}, u32[]{:S(2)}) collective-permute-start(f32[24,128]{1,0:T(8,128)S(1)} %shard_map.145.r_0_), channel_id=1, source_target_pairs={{0,1},{1,0},{2,3},{3,2},{4,5},{5,4},{6,7},{7,6},{8,9},{9,8},{10,11... | collective-permute-start | bytes 36872 | tf_op jit(solution)/shard_map/ppermute | solution.py:77
  34.8 5.6 %collective-permute-start.13 = (f32[24,128]{1,0:T(8,128)S(1)}, f32[24,128]{1,0:T(8,128)S(1)}, u32[]{:S(2)}, u32[]{:S(2)}) collective-permute-start(f32[24,128]{1,0:T(8,128)S(1)} %shard_map.145.r_0_), channel_id=1, source_target_pairs={{0,2},{1,3},{2,0},{3,1},{4,6},{5,7},{6,4},{7,5},{8,10},{9,11},{10,... | collective-permute-start | bytes 36872 | tf_op jit(solution)/shard_map/ppermute | solution.py:77
  38.6 5.5 %collective-permute-start.14 = (f32[24,128]{1,0:T(8,128)S(1)}, f32[24,128]{1,0:T(8,128)S(1)}, u32[]{:S(2)}, u32[]{:S(2)}) collective-permute-start(f32[24,128]{1,0:T(8,128)S(1)} %shard_map.145.r_0_), channel_id=1, source_target_pairs={{0,3},{1,2},{2,1},{3,0},{4,7},{5,6},{6,5},{7,4},{8,11},{9,10},{10,... | collective-permute-start | bytes 36872 | tf_op jit(solution)/shard_map/ppermute | solution.py:77
  45.1 1.3 %collective-permute-start.15 = (f32[40,128]{1,0:T(8,128)S(1)}, f32[40,128]{1,0:T(8,128)S(1)}, u32[]{:S(2)}, u32[]{:S(2)}) collective-permute-start(f32[40,128]{1,0:T(8,128)S(1)} %get-tuple-element.49.r_0_), channel_id=1, source_target_pairs={{0,4},{4,0},{8,12},{12,8},{16,20},{20,16},{24,28},{28,24},{1,5},{5... | collective-permute-start | bytes 61448 | tf_op jit(solution)/shard_map/ppermute | solution.py:71
  45.2 4.2 %collective-permute-start.16 = (f32[40,128]{1,0:T(8,128)S(1)}, f32[40,128]{1,0:T(8,128)S(1)}, u32[]{:S(2)}, u32[]{:S(2)}) collective-permute-start(f32[40,128]{1,0:T(8,128)S(1)} %get-tuple-element.49.r_0_), channel_id=1, source_target_pairs={{0,28},{4,8},{8,4},{12,16},{16,12},{20,24},{24,20},{28,0},{1,29},{... | collective-permute-start | bytes 61448 | tf_op jit(solution)/shard_map/ppermute | solution.py:71
  50.5 5.6 %collective-permute-start.17 = (f32[20,128]{1,0:T(8,128)S(1)}, f32[20,128]{1,0:T(8,128)S(1)}, u32[]{:S(2)}, u32[]{:S(2)}) collective-permute-start(f32[20,128]{1,0:T(8,128)S(1)} %get-tuple-element.51), channel_id=1, source_target_pairs={{0,1},{1,0},{2,3},{3,2},{4,5},{5,4},{6,7},{7,6},{8,9},{9,8},{10,11... | collective-permute-start | bytes 30728 | tf_op jit(solution)/shard_map/ppermute | solution.py:77
  50.6 5.5 %collective-permute-start.18 = (f32[20,128]{1,0:T(8,128)S(1)}, f32[20,128]{1,0:T(8,128)S(1)}, u32[]{:S(2)}, u32[]{:S(2)}) collective-permute-start(f32[20,128]{1,0:T(8,128)S(1)} %get-tuple-element.52), channel_id=1, source_target_pairs={{0,2},{1,3},{2,0},{3,1},{4,6},{5,7},{6,4},{7,5},{8,10},{9,11},{10,... | collective-permute-start | bytes 30728 | tf_op jit(solution)/shard_map/ppermute | solution.py:77
  51.6 5.5 %collective-permute-start.19 = (f32[20,128]{1,0:T(8,128)S(1)}, f32[20,128]{1,0:T(8,128)S(1)}, u32[]{:S(2)}, u32[]{:S(2)}) collective-permute-start(f32[20,128]{1,0:T(8,128)S(1)} %get-tuple-element.53), channel_id=1, source_target_pairs={{0,3},{1,2},{2,1},{3,0},{4,7},{5,6},{6,5},{7,4},{8,11},{9,10},{10,... | collective-permute-start | bytes 30728 | tf_op jit(solution)/shard_map/ppermute | solution.py:77
where the time goes:
time: 58.5 us; the launch traced here: 58.2 us
  starting transfers between devices  25.5 us (44%)
  waiting for transfers between devices  21.7 us (37%)
  Pallas kernels  10.2 us (17%)
  between operations  0.77 us (1%)
    ppermute x12, starting transfers between devices, col_exchange(): got.append(lax.ppermute(pieces[j], 'col', col_pairs(j)))  17.7 us
    ppermute x12, waiting for transfers between devices, col_exchange(): got.append(lax.ppermute(pieces[j], 'col', col_pairs(j)))  11.6 us
    pallas_call x11, Pallas kernels, call(): pl.pallas_call(kernel, out_shape=[kind(*o) for o in out] if many else kin...  10.2 us
    ppermute x8, waiting for transfers between devices, sec_exchange(): return [lax.ppermute(x, 'sec', pairs) for pairs in sec_partners()]  10.2 us
    ppermute x8, starting transfers between devices, sec_exchange(): return [lax.ppermute(x, 'sec', pairs) for pairs in sec_partners()]  7.83 us
  transfers between devices with their start and end apart: 20, of which 10 were waited for; matrix products, arithmetic and copies ran while one was open for 0% of the time, Pallas kernels for 6%

commit v1 on v0

--- a/solution.py
+++ b/solution.py
@@ -68,7 +68,10 @@
 
 
 def sec_exchange(x):
-    return [lax.ppermute(x, "sec", pairs) for pairs in sec_partners()]
+    got = []
+    for pairs in sec_partners():
+        got.append(lax.ppermute(x, "sec", pairs))
+    return got
 
 
 def col_exchange(pieces):
@@ -151,28 +154,31 @@
     return copies
 
 
-def first_kernel(cols, secs, cells_here, cols_here,
-                 sea_ref, ice_hbm, air_ref, src_hbm, w_hbm, forcing_hbm, mask_hbm, feed_hbm, feed_w_hbm, wet_hbm,
-                 top_ref, code_ref, fixed_ref, feed_ref, ice_ref, wet_ref,
-                 sea0, air0, src_ref, w_ref, forcing_ref, mask_ref, feed_in, feed_w, sems):
-    tiles, sea_tiles = mask_ref.shape[0], ice_ref.shape[0]
+def first_top(sea_hbm, ice_hbm, top_ref, sea0, sems):
+    n = ice_hbm.shape[0]
+    copies = fetch([(sea_hbm.at[0, pl.ds(0, SUBS * n)], sea0), (ice_hbm, top_ref.at[pl.ds(n, n)])], sems)
+    for c in copies:
+        c.wait()
+    top_ref[0:n] = sea0[level_rows(0, n), :]
+
+
+def first_rest(cols, secs, cells_here, cols_here,
+               air_hbm, src_hbm, w_hbm, forcing_hbm, mask_hbm, feed_hbm, feed_w_hbm, wet_hbm,
+               code_ref, fixed_ref, feed_ref, wet_ref,
+               air0, src_ref, w_ref, forcing_ref, mask_ref, feed_in, sems):
+    tiles = mask_ref.shape[0]
+    m = feed_in.shape[0]
     sec, col = lax.axis_index("sec"), lax.axis_index("col")
     copies = fetch(
-        [(sea_ref.at[0, pl.ds(0, SUBS * sea_tiles)], sea0), (ice_hbm, ice_ref), (feed_hbm, feed_in), (feed_w_hbm, feed_w),
+        [(feed_hbm, feed_in), (feed_w_hbm, feed_ref.at[pl.ds(m, m)]),
          (src_hbm, src_ref), (w_hbm, w_ref), (forcing_hbm, forcing_ref), (mask_hbm, mask_ref), (wet_hbm, wet_ref),
-         (air_ref.at[:, pl.ds(0, SUBS * tiles)], air0)], sems)
+         (air_hbm.at[:, pl.ds(0, SUBS * tiles)], air0)], sems)
     for c in copies:
         c.wait()
-    top_ref[0:sea_tiles] = sea0[level_rows(0, sea_tiles), :]
-    top_ref[sea_tiles:] = ice_ref[...]
-
-    s = feed_in[...]
-    band, within = split(s, cols_here * cols)
+    band, within = split(feed_in[...], cols_here * cols)
     owner, place = split(within, cols_here)
     code = (owner * 3 + section_slot(band, sec, secs)) * cols_here + place
-    m = s.shape[0]
     feed_ref[0:m] = code.astype(jnp.float32)
-    feed_ref[m : 2 * m] = feed_w[...]
 
     mask = mask_ref[...] == 1
     ks = src_ref.shape[0] // tiles
@@ -287,17 +293,16 @@
         his.append(hi)
         lanes.append(lane)
         vals.append([jnp.zeros(lane.shape, jnp.float32) for _ in range(2)])
-    for slot in range(3):
-        for j in range(pieces):
-            for r in range(cell_rows):
-                number = (slot * pieces + j) * cell_rows + r
-                base = slot * 2 * cell_rows + r
-                row0 = tables[j][base : base + 1, :]
-                row1 = tables[j][base + cell_rows : base + cell_rows + 1, :]
-                for k in range(ks):
-                    hit = his[k] == number
-                    vals[k][0] = jnp.where(hit, lane_gather(row0, lanes[k]), vals[k][0])
-                    vals[k][1] = jnp.where(hit, lane_gather(row1, lanes[k]), vals[k][1])
+    for k in range(ks):
+        for slot in range(3):
+            for j in range(pieces):
+                for r in range(cell_rows):
+                    hit = his[k] == (slot * pieces + j) * cell_rows + r
+                    base = slot * 2 * cell_rows + r
+                    for v in range(2):
+                        at = base + v * cell_rows
+                        found = lane_gather(tables[j][at : at + 1, :], lanes[k])
+                        vals[k][v] = jnp.where(hit, found, vals[k][v])
     skin = fixed_ref[ks + 3]
     frozen = jnp.zeros_like(skin)
     for k in range(ks):
@@ -327,9 +332,10 @@
         add_ref[v] = value
 
 
-def partial_kernel(pieces, offset, *refs):
-    flux, refs = refs[:3], refs[3:]
-    bundles, outs = refs[:pieces], refs[pieces:]
+def partial_kernel(offset, slots, pieces, *refs):
+    flux, refs = refs[: len(slots)], refs[len(slots) :]
+    bundles, refs = refs[:pieces], refs[pieces:]
+    before, outs = refs[:-pieces], refs[-pieces:]
     col_rows = flux[0].shape[0] // FLUXES
     base = lax.axis_index("col") * (3 * col_rows)
     m = outs[0].shape[0] // FLUXES
@@ -347,26 +353,30 @@
             hi, lane = split(code, LANES)
             hi = hi - base
             vals = [jnp.zeros(lane.shape, jnp.float32) for _ in range(FLUXES)]
-            for slot in range(3):
+            for table, slot in zip(flux, slots):
                 for r in range(col_rows):
                     hit = hi == slot * col_rows + r
                     for v in range(FLUXES):
-                        row = flux[slot][v * col_rows + r : v * col_rows + r + 1, :]
+                        row = table[v * col_rows + r : v * col_rows + r + 1, :]
                         vals[v] = jnp.where(hit, lane_gather(row, lane), vals[v])
             for v in range(FLUXES):
                 part = w * vals[v]
                 total[v] = part if total[v] is None else total[v] + part
         for v in range(FLUXES):
+            at = slice(v * m, (v + 1) * m)
             whole = total[v][0:m]
             for p in range(1, per):
                 whole = whole + total[v][p * m : (p + 1) * m]
-            outs[j][v * m : (v + 1) * m] = whole
+            outs[j][at] = whole + before[j][at] if before else whole
 
 
 def sea_kernel(pieces, depth, last, *refs):
     parts, refs = refs[:pieces], refs[pieces:]
     state_ref, mix_ref, ice_ref, mask_ref, refs = refs[0], refs[1], refs[2], refs[3], refs[4:]
-    out_ref, top_ref, fac, work = refs
+    if last:
+        out_hbm, top_hbm, fac, work, out_ref, top_ref, sems = refs
+    else:
+        out_ref, top_ref, fac, work = refs
     tiles = mix_ref.shape[0] // depth
     flux = []
     for v in range(FLUXES):
@@ -397,6 +407,13 @@
         if back is not None:
             fac[2, i] = back
 
+    copies = []
+    if last:
+        top_ref[...] = new_ice
+        copies.append(pltpu.make_async_copy(top_ref, top_hbm, sems.at[2]))
+        copies[-1].start()
+    else:
+        top_ref[tiles : 2 * tiles] = new_ice
     middle = factor(mix, depth, put)
     for f in range(2):
         def rhs(i, f=f):
@@ -416,10 +433,11 @@
                 top_ref[0:tiles] = new
 
         apply_factor(rhs, depth, lambda i: (fac[0, i], fac[1, i], fac[2, i]), middle, keep, kept, store)
-    if last:
-        top_ref[...] = new_ice
-    else:
-        top_ref[tiles : 2 * tiles] = new_ice
+        if last:
+            copies.append(pltpu.make_async_copy(out_ref.at[f], out_hbm.at[f], sems.at[f]))
+            copies[-1].start()
+    for c in copies:
+        c.wait()
 
 
 def air_finish(y2_ref, hg_ref, first_ref, second_ref, out_ref):
@@ -434,17 +452,16 @@
                 out_ref[f, at] = y2_ref[f, at] + hg_ref[0, at] * b1 + hg_ref[1, at] * b2
 
 
-def call(kernel, out, *args, scratch=(), final=False, raw=False):
-    many = isinstance(out, list)
-    kind = jax.ShapeDtypeStruct if final else pltpu.VMEM
+def call(kernel, out, *args, scratch=(), out_space=pltpu.VMEM, space=pltpu.VMEM):
+    spaces = out_space if isinstance(out_space, list) else [out_space] * len(out)
     return pl.pallas_call(
         kernel,
-        out_shape=[kind(*o) for o in out] if many else kind(*out),
-        in_specs=[pl.BlockSpec(memory_space=pltpu.HBM if raw else pltpu.VMEM)] * len(args),
-        out_specs=[pl.BlockSpec(memory_space=pltpu.VMEM)] * len(out) if many else pl.BlockSpec(memory_space=pltpu.VMEM),
+        out_shape=[pltpu.VMEM(*o) if sp is pltpu.VMEM else jax.ShapeDtypeStruct(*o) for o, sp in zip(out, spaces)],
+        in_specs=[pl.BlockSpec(memory_space=space)] * len(args),
+        out_specs=[pl.BlockSpec(memory_space=sp or pltpu.VMEM) for sp in spaces],
         scratch_shapes=list(scratch),
         compiler_params=pltpu.CompilerParams(vmem_limit_bytes=8 << 20),
-    )(*[pltpu.with_memory_space_constraint(a, pltpu.HBM if raw else pltpu.VMEM) for a in args])
+    )(*[pltpu.with_memory_space_constraint(a, space) for a in args])
 
 
 def per_device(air_state, air_mix, surface_forcing, air_mask, ocean_sources, ocean_weights,
@@ -467,22 +484,25 @@
     feed_rows = 2 * air_sources.shape[0] * sea_tiles
     smalls = [tile_rows(v) for v in (ocean_sources, ocean_weights, surface_forcing)]
     feeds = [tile_rows(v) for v in (air_sources, air_weights)]
-    top, code, fixed, feed, ice, wet = call(
-        lambda *r: first_kernel(cols, secs, cells, here, *r),
-        [((2 * sea_tiles, LANES), f32), ((ko, tiles, LANES), i32), ((ko + 8, tiles, LANES), f32),
-         ((feed_rows, LANES), f32), (ice.shape, f32), (wet.shape, i32)],
-        sea, ice, air, *smalls, air_mask.reshape(tiles, LANES), *feeds, wet, raw=True,
-        scratch=[pltpu.VMEM((SUBS * sea_tiles, LANES), f32), pltpu.VMEM((fields, SUBS * tiles, LANES), f32),
-                 *[pltpu.VMEM(v.shape, v.dtype) for v in smalls], pltpu.VMEM((tiles, LANES), i32),
-                 *[pltpu.VMEM(v.shape, v.dtype) for v in feeds], pltpu.SemaphoreType.DMA((10,))],
+    hbm = pltpu.HBM
+    vmem = lambda v: pltpu.VMEM(v.shape, v.dtype)
+    (top,) = call(first_top, [((2 * sea_tiles, LANES), f32)], sea, ice, space=hbm,
+                  scratch=[pltpu.VMEM((SUBS * sea_tiles, LANES), f32), pltpu.SemaphoreType.DMA((2,))])
+    near = sec_exchange(top)
+    code, fixed, feed, wet = call(
+        lambda *r: first_rest(cols, secs, cells, here, *r),
+        [((ko, tiles, LANES), i32), ((ko + 8, tiles, LANES), f32), ((feed_rows, LANES), f32), (wet.shape, i32)],
+        air, *smalls, air_mask.reshape(tiles, LANES), *feeds, wet, space=hbm,
+        scratch=[pltpu.VMEM((fields, SUBS * tiles, LANES), f32), *map(vmem, smalls), pltpu.VMEM((tiles, LANES), i32),
+                 vmem(feeds[0]), pltpu.SemaphoreType.DMA((8,))],
     )
-    near = sec_exchange(top)
-    bundle = call(first_bundle, ((offset + feed_rows, LANES), f32), top, *near, feed)
+    ice = top[sea_tiles:]
+    (bundle,) = call(first_bundle, [((offset + feed_rows, LANES), f32)], top, *near, feed)
     y2, hg, tops, sea, sea_k = call(
         air_prepare,
         [(air.shape, f32), ((2,) + mixing.shape, f32), ((fields + 1, tiles, LANES), f32), (sea.shape, f32), (sea_k.shape, f32)],
-        air, mixing, sea, sea_k, raw=True,
-        scratch=[pltpu.VMEM(air.shape, f32), pltpu.VMEM(mixing.shape, f32), pltpu.VMEM((3, levels, tiles, LANES), f32),
+        air, mixing, sea, sea_k, space=hbm,
+        scratch=[vmem(air), vmem(mixing), pltpu.VMEM((3, levels, tiles, LANES), f32),
                  pltpu.VMEM((fields + 1, levels, tiles, LANES), f32), pltpu.VMEM((fields + 1, levels, tiles, LANES), f32),
                  pltpu.SemaphoreType.DMA((fields + 3,))],
     )
@@ -496,24 +516,28 @@
             *tables, code, fixed, *extra,
         )
         adds.append(add)
-        parts = call(
-            lambda *r: partial_kernel(cols, offset, *r),
-            [((FLUXES * sea_tiles, LANES), f32)] * cols,
-            flux, *sec_exchange(flux), *bundles,
-        )
-        moved = col_exchange(parts)
+        near = sec_exchange(flux)
+        share = ((FLUXES * sea_tiles, LANES), f32)
+        sums = lambda slots, peers, *args: call(
+            lambda *r: partial_kernel(offset, slots, len(peers), *r), [share] * len(peers), *args)
+        parts = sums((0,), bundles[1:], flux, *bundles[1:])
+        parts = sums((1,), bundles[1:], near[0], *bundles[1:], *parts)
+        parts = sums((2,), bundles[1:], near[1], *bundles[1:], *parts)
+        moved = col_exchange([flux, *parts])
+        moved[:1] = sums((0, 1, 2), bundles[:1], flux, *near, bundles[0])
         last = step == STEPS - 1
         if last:
-            air_out = call(air_finish, (air.shape, f32), y2, hg, *adds, final=True)
+            (air_out,) = call(air_finish, [(air.shape, f32)], y2, hg, *adds, out_space=None)
+        solve_scratch = [pltpu.VMEM((3, depth, sea_tiles, LANES), f32), pltpu.VMEM((2, depth, sea_tiles, LANES), f32)]
         sea, top = call(
             lambda *r: sea_kernel(cols, depth, last, *r),
             [(sea.shape, f32), ((sea_tiles if last else 2 * sea_tiles, LANES), f32)],
-            *moved, sea, sea_k, ice, wet, final=last,
-            scratch=[pltpu.VMEM((3, depth, sea_tiles, LANES), f32), pltpu.VMEM((2, depth, sea_tiles, LANES), f32)],
+            *moved, sea, sea_k, ice, wet, out_space=hbm if last else pltpu.VMEM,
+            scratch=solve_scratch + ([vmem(sea), vmem(ice), pltpu.SemaphoreType.DMA((3,))] if last else []),
         )
         if not last:
             ice = top[sea_tiles:]
-            bundle = call(later_bundle, ((offset, LANES), f32), top, *sec_exchange(top))
+            (bundle,) = call(later_bundle, [((offset, LANES), f32)], top, *sec_exchange(top))
             tables = col_exchange([bundle] * cols)
     return (untile_rows(air_out, levels, here), untile_rows(sea, depth, cells), top.reshape(cells))
 

time: 58.5 us -> 55.8 us (0.954)
  waiting for transfers between devices: 21.7 us -> 19.1 us
    ppermute x8, waiting for transfers between devices: 10.2 us -> 7.93 us  [sec_exchange(): got.append(lax.ppermute(x, 'sec', pairs))]
    pallas_call x11 -> x18, Pallas kernels: 10.2 us -> 10.4 us  [call(): pl.pallas_call(kernel, out_shape=[pltpu.VMEM(*o) if sp is pltpu.VMEM else...]
  transfers between devices with their start and end apart: 20 -> 20, of which waited for: 10 -> 11; matrix products, arithmetic and copies ran while one was open for 0% -> 0% of each run, Pallas kernels for 6% -> 12%
where the time goes in v1:
time: 55.8 us; the launch traced here: 55.5 us
  starting transfers between devices  25.2 us (45%)
  waiting for transfers between devices  19.1 us (34%)
  Pallas kernels  10.4 us (19%)
  between operations  0.84 us (2%)
    ppermute x12, starting transfers between devices, col_exchange(): got.append(lax.ppermute(pieces[j], 'col', col_pairs(j)))  17.7 us
    ppermute x12, waiting for transfers between devices, col_exchange(): got.append(lax.ppermute(pieces[j], 'col', col_pairs(j)))  11.2 us
    pallas_call x18, Pallas kernels, call(): pl.pallas_call(kernel, out_shape=[pltpu.VMEM(*o) if sp is pltpu.VMEM else...  10.4 us
    ppermute x8, waiting for transfers between devices, sec_exchange(): got.append(lax.ppermute(x, 'sec', pairs))  7.93 us
    ppermute x8, starting transfers between devices, sec_exchange(): got.append(lax.ppermute(x, 'sec', pairs))  7.51 us
  transfers between devices with their start and end apart: 20, of which 11 were waited for; matrix products, arithmetic and copies ran while one was open for 0% of the time, Pallas kernels for 12%

profile of v1, /device:TPU:0, one launch (start us, length us, event | category | flops | bytes accessed | tf_op | source)
XLA Modules:
  0.0 55.5 jit_solution(9972873863036840841)
XLA Ops:
  0.6 0.7 %shard_map.140.own_ref = f32[8,128]{1,0:T(8,128)S(1)} custom-call(f32[2,320,128]{2,1,0:T(8,128)} %bitcast.61, f32[4,128]{1,0:T(4,128)} %bitcast.72), custom_call_target="tpu_custom_call" | custom-call | tf_op jit(solution)/shard_map/pallas_call | solution.py:457
  1.9 3.5 %collective-permute-start.1 = (f32[8,128]{1,0:T(8,128)S(1)}, f32[8,128]{1,0:T(8,128)S(1)}, u32[]{:S(2)}, u32[]{:S(2)}) collective-permute-start(f32[8,128]{1,0:T(8,128)S(1)} %shard_map.140.own_ref), channel_id=1, source_target_pairs={{0,28},{4,8},{8,4},{12,16},{16,12},{20,24},{24,20},{28,0},{1,29},{... | collective-permute-start | bytes 12296 | tf_op jit(solution)/shard_map/ppermute | solution.py:73
  5.5 1.1 %shard_map.141 = (s32[4,8,128]{2,1,0:T(8,128)S(1)}, f32[12,8,128]{2,1,0:T(8,128)S(1)}, f32[32,128]{1,0:T(8,128)S(1)}, s32[4,128]{1,0:T(4,128)S(1)}) custom-call(f32[4,512,128]{2,1,0:T(8,128)} %bitcast.59, s32[32,128]{1,0:T(8,128)} %bitcast.66, f32[32,128]{1,0:T(8,128)} %bitcast.67, f32[32,128]{1,0:T(8,128)} %bitcast.68, s32[8,128]{1,0:T(8,128)} %bitcast.71, ...), custom_call_target="tpu_custom_call" | custom-call | tf_op jit(solution)/shard_map/pallas_call | solution.py:457
  6.8 1.7 %collective-permute-start.2 = (f32[56,128]{1,0:T(8,128)S(1)}, f32[56,128]{1,0:T(8,128)S(1)}, u32[]{:S(2)}, u32[]{:S(2)}) collective-permute-start(f32[56,128]{1,0:T(8,128)S(1)} %shard_map.142.r_0_.r_3_), channel_id=1, source_target_pairs={{0,1},{1,0},{2,3},{3,2},{4,5},{5,4},{6,7},{7,6},{8,9},{9,8},{10,11... | collective-permute-start | bytes 86024 | tf_op jit(solution)/shard_map/ppermute | solution.py:80
  8.5 2.6 %collective-permute-start.3 = (f32[56,128]{1,0:T(8,128)S(1)}, f32[56,128]{1,0:T(8,128)S(1)}, u32[]{:S(2)}, u32[]{:S(2)}) collective-permute-start(f32[56,128]{1,0:T(8,128)S(1)} %shard_map.142.r_0_.r_3_), channel_id=1, source_target_pairs={{0,2},{1,3},{2,0},{3,1},{4,6},{5,7},{6,4},{7,5},{8,10},{9,11},{10,... | collective-permute-start | bytes 86024 | tf_op jit(solution)/shard_map/ppermute | solution.py:80
  11.2 2.5 %collective-permute-done.3.r_2_ = f32[56,128]{1,0:T(8,128)S(1)} collective-permute-done((f32[56,128]{1,0:T(8,128)S(1)}, f32[56,128]{1,0:T(8,128)S(1)}, u32[]{:S(2)}, u32[]{:S(2)}) %collective-permute-start.3) | collective-permute-done | bytes 28704 | tf_op jit(solution)/shard_map/ppermute | solution.py:80
  13.8 3.0 %collective-permute-done.4.r_3_ = f32[56,128]{1,0:T(8,128)S(1)} collective-permute-done((f32[56,128]{1,0:T(8,128)S(1)}, f32[56,128]{1,0:T(8,128)S(1)}, u32[]{:S(2)}, u32[]{:S(2)}) %collective-permute-start.4) | collective-permute-done | bytes 28704 | tf_op jit(solution)/shard_map/ppermute | solution.py:80
  17.4 1.8 %collective-permute-start.6 = (f32[40,128]{1,0:T(8,128)S(1)}, f32[40,128]{1,0:T(8,128)S(1)}, u32[]{:S(2)}, u32[]{:S(2)}) collective-permute-start(f32[40,128]{1,0:T(8,128)S(1)} %get-tuple-element.44.r_0_), channel_id=1, source_target_pairs={{0,28},{4,8},{8,4},{12,16},{16,12},{20,24},{24,20},{28,0},{1,29},{... | collective-permute-start | bytes 61448 | tf_op jit(solution)/shard_map/ppermute | solution.py:73
  19.8 1.7 %collective-permute-done.6.r_2_.r_0_ = f32[40,128]{1,0:T(8,128)S(1)} collective-permute-done((f32[40,128]{1,0:T(8,128)S(1)}, f32[40,128]{1,0:T(8,128)S(1)}, u32[]{:S(2)}, u32[]{:S(2)}) %collective-permute-start.6) | collective-permute-done | bytes 20512 | tf_op jit(solution)/shard_map/ppermute | solution.py:73
  22.0 0.9 %collective-permute-start.8 = (f32[20,128]{1,0:T(8,128)S(1)}, f32[20,128]{1,0:T(8,128)S(1)}, u32[]{:S(2)}, u32[]{:S(2)}) collective-permute-start(f32[20,128]{1,0:T(8,128)S(1)} %get-tuple-element.52), channel_id=1, source_target_pairs={{0,2},{1,3},{2,0},{3,1},{4,6},{5,7},{6,4},{7,5},{8,10},{9,11},{10,... | collective-permute-start | bytes 30728 | tf_op jit(solution)/shard_map/ppermute | solution.py:80
  22.8 3.5 %collective-permute-start.9 = (f32[20,128]{1,0:T(8,128)S(1)}, f32[20,128]{1,0:T(8,128)S(1)}, u32[]{:S(2)}, u32[]{:S(2)}) collective-permute-start(f32[20,128]{1,0:T(8,128)S(1)} %get-tuple-element.53), channel_id=1, source_target_pairs={{0,3},{1,2},{2,1},{3,0},{4,7},{5,6},{6,5},{7,4},{8,11},{9,10},{10,... | collective-permute-start | bytes 30728 | tf_op jit(solution)/shard_map/ppermute | solution.py:80
  26.3 2.1 %shard_map.139 = (f32[4,512,128]{2,1,0:T(8,128)S(1)}, f32[2,512,128]{2,1,0:T(8,128)S(1)}, f32[5,8,128]{2,1,0:T(8,128)S(1)}, f32[2,320,128]{2,1,0:T(8,128)S(1)}, f32[320,128]{1,0:T(8,128)S(1)}) custom-call(f32[4,512,128]{2,1,0:T(8,128)} %bitcast.60, f32[512,128]{1,0:T(8,128)} %bitcast.64, f32[2,320,128]{2,1,0:T(8,128)} %bitcast.62, f32[320,128]{1,0:T(8,128)} %bitcast.65), custom_call_target="tpu_custom_call" | custom-call | tf_op jit(solution)/shard_map/pallas_call | solution.py:457
  29.3 0.9 %collective-permute-start.11 = (f32[8,128]{1,0:T(8,128)S(1)}, f32[8,128]{1,0:T(8,128)S(1)}, u32[]{:S(2)}, u32[]{:S(2)}) collective-permute-start(f32[8,128]{1,0:T(8,128)S(1)} %get-tuple-element.57.own_ref), channel_id=1, source_target_pairs={{0,28},{4,8},{8,4},{12,16},{16,12},{20,24},{24,20},{28,0},{1,29},{... | collective-permute-start | bytes 12296 | tf_op jit(solution)/shard_map/ppermute | solution.py:73
  30.4 2.8 %collective-permute-done.11.m2_ref = f32[8,128]{1,0:T(8,128)S(1)} collective-permute-done((f32[8,128]{1,0:T(8,128)S(1)}, f32[8,128]{1,0:T(8,128)S(1)}, u32[]{:S(2)}, u32[]{:S(2)}) %collective-permute-start.11) | collective-permute-done | bytes 4128 | tf_op jit(solution)/shard_map/ppermute | solution.py:73
  33.3 3.6 %collective-permute-start.13 = (f32[24,128]{1,0:T(8,128)S(1)}, f32[24,128]{1,0:T(8,128)S(1)}, u32[]{:S(2)}, u32[]{:S(2)}) collective-permute-start(f32[24,128]{1,0:T(8,128)S(1)} %shard_map.149.r_0_), channel_id=1, source_target_pairs={{0,2},{1,3},{2,0},{3,1},{4,6},{5,7},{6,4},{7,5},{8,10},{9,11},{10,... | collective-permute-start | bytes 36872 | tf_op jit(solution)/shard_map/ppermute | solution.py:80
  36.9 0.8 %collective-permute-start.14 = (f32[24,128]{1,0:T(8,128)S(1)}, f32[24,128]{1,0:T(8,128)S(1)}, u32[]{:S(2)}, u32[]{:S(2)}) collective-permute-start(f32[24,128]{1,0:T(8,128)S(1)} %shard_map.149.r_0_), channel_id=1, source_target_pairs={{0,3},{1,2},{2,1},{3,0},{4,7},{5,6},{6,5},{7,4},{8,11},{9,10},{10,... | collective-permute-start | bytes 36872 | tf_op jit(solution)/shard_map/ppermute | solution.py:80
  37.7 1.0 %collective-permute-done.13.r_2_ = f32[24,128]{1,0:T(8,128)S(1)} collective-permute-done((f32[24,128]{1,0:T(8,128)S(1)}, f32[24,128]{1,0:T(8,128)S(1)}, u32[]{:S(2)}, u32[]{:S(2)}) %collective-permute-start.13) | collective-permute-done | bytes 12320 | tf_op jit(solution)/shard_map/ppermute | solution.py:80
  38.6 3.7 %collective-permute-done.14.r_3_ = f32[24,128]{1,0:T(8,128)S(1)} collective-permute-done((f32[24,128]{1,0:T(8,128)S(1)}, f32[24,128]{1,0:T(8,128)S(1)}, u32[]{:S(2)}, u32[]{:S(2)}) %collective-permute-start.14) | collective-permute-done | bytes 12320 | tf_op jit(solution)/shard_map/ppermute | solution.py:80
  44.5 2.6 %collective-permute-done.16.r_2_.r_0_ = f32[40,128]{1,0:T(8,128)S(1)} collective-permute-done((f32[40,128]{1,0:T(8,128)S(1)}, f32[40,128]{1,0:T(8,128)S(1)}, u32[]{:S(2)}, u32[]{:S(2)}) %collective-permute-start.16) | collective-permute-done | bytes 20512 | tf_op jit(solution)/shard_map/ppermute | solution.py:73
  47.6 1.4 %collective-permute-start.18 = (f32[20,128]{1,0:T(8,128)S(1)}, f32[20,128]{1,0:T(8,128)S(1)}, u32[]{:S(2)}, u32[]{:S(2)}) collective-permute-start(f32[20,128]{1,0:T(8,128)S(1)} %get-tuple-element.68), channel_id=1, source_target_pairs={{0,2},{1,3},{2,0},{3,1},{4,6},{5,7},{6,4},{7,5},{8,10},{9,11},{10,... | collective-permute-start | bytes 30728 | tf_op jit(solution)/shard_map/ppermute | solution.py:80
  48.9 3.0 %collective-permute-start.19 = (f32[20,128]{1,0:T(8,128)S(1)}, f32[20,128]{1,0:T(8,128)S(1)}, u32[]{:S(2)}, u32[]{:S(2)}) collective-permute-start(f32[20,128]{1,0:T(8,128)S(1)} %get-tuple-element.69), channel_id=1, source_target_pairs={{0,3},{1,2},{2,1},{3,0},{4,7},{5,6},{6,5},{7,4},{8,11},{9,10},{10,... | collective-permute-start | bytes 30728 | tf_op jit(solution)/shard_map/ppermute | solution.py:80
  51.9 1.2 %shard_map.151 = f32[4,512,128]{2,1,0:T(8,128)} custom-call(f32[4,512,128]{2,1,0:T(8,128)S(1)} %get-tuple-element.38.y2_ref, f32[2,512,128]{2,1,0:T(8,128)S(1)} %get-tuple-element.39.hg_ref, f32[4,8,128]{2,1,0:T(8,128)S(1)} %get-tuple-element.43.r_7_.first_ref, f32[4,8,128]{2,1,0:T(8,128)S(1)} %get-tuple-element.59.second_ref), custom_call_target="tpu_custom_call" | custom-call | tf_op jit(solution)/shard_map/pallas_call | solution.py:457
  53.5 0.9 %collective-permute-done.19.r_3_ = f32[20,128]{1,0:T(8,128)S(1)} collective-permute-done((f32[20,128]{1,0:T(8,128)S(1)}, f32[20,128]{1,0:T(8,128)S(1)}, u32[]{:S(2)}, u32[]{:S(2)}) %collective-permute-start.19) | collective-permute-done | bytes 10272 | tf_op jit(solution)/shard_map/ppermute | solution.py:80
  54.4 1.1 %shard_map.156 = (f32[2,320,128]{2,1,0:T(8,128)}, f32[4,128]{1,0:T(4,128)}) custom-call(f32[20,128]{1,0:T(8,128)S(1)} %shard_map.152.r_0_, f32[20,128]{1,0:T(8,128)S(1)} %collective-permute-done.17.r_1_, f32[20,128]{1,0:T(8,128)S(1)} %collective-permute-done.18.r_2_, f32[20,128]{1,0:T(8,128)S(1)} %collective-permute-done.19.r_3_, ...), custom_call_target="tpu_custom_call" | custom-call | tf_op jit(solution)/shard_map/pallas_call | solution.py:457
  (36 shorter events, 6.5 us)
Async XLA Ops:
  1.4 5.2 %collective-permute-start = (f32[8,128]{1,0:T(8,128)S(1)}, f32[8,128]{1,0:T(8,128)S(1)}, u32[]{:S(2)}, u32[]{:S(2)}) collective-permute-start(f32[8,128]{1,0:T(8,128)S(1)} %shard_map.140.own_ref), channel_id=1, source_target_pairs={{0,4},{4,0},{8,12},{12,8},{16,20},{20,16},{24,28},{28,24},{1,5},{5... | collective-permute-start | bytes 12296 | tf_op jit(solution)/shard_map/ppermute | solution.py:73
  1.9 4.9 %collective-permute-start.1 = (f32[8,128]{1,0:T(8,128)S(1)}, f32[8,128]{1,0:T(8,128)S(1)}, u32[]{:S(2)}, u32[]{:S(2)}) collective-permute-start(f32[8,128]{1,0:T(8,128)S(1)} %shard_map.140.own_ref), channel_id=1, source_target_pairs={{0,28},{4,8},{8,4},{12,16},{16,12},{20,24},{24,20},{28,0},{1,29},{... | collective-permute-start | bytes 12296 | tf_op jit(solution)/shard_map/ppermute | solution.py:73
  6.8 4.4 %collective-permute-start.2 = (f32[56,128]{1,0:T(8,128)S(1)}, f32[56,128]{1,0:T(8,128)S(1)}, u32[]{:S(2)}, u32[]{:S(2)}) collective-permute-start(f32[56,128]{1,0:T(8,128)S(1)} %shard_map.142.r_0_.r_3_), channel_id=1, source_target_pairs={{0,1},{1,0},{2,3},{3,2},{4,5},{5,4},{6,7},{7,6},{8,9},{9,8},{10,11... | collective-permute-start | bytes 86024 | tf_op jit(solution)/shard_map/ppermute | solution.py:80
  8.5 5.2 %collective-permute-start.3 = (f32[56,128]{1,0:T(8,128)S(1)}, f32[56,128]{1,0:T(8,128)S(1)}, u32[]{:S(2)}, u32[]{:S(2)}) collective-permute-start(f32[56,128]{1,0:T(8,128)S(1)} %shard_map.142.r_0_.r_3_), channel_id=1, source_target_pairs={{0,2},{1,3},{2,0},{3,1},{4,6},{5,7},{6,4},{7,5},{8,10},{9,11},{10,... | collective-permute-start | bytes 86024 | tf_op jit(solution)/shard_map/ppermute | solution.py:80
  11.1 5.7 %collective-permute-start.4 = (f32[56,128]{1,0:T(8,128)S(1)}, f32[56,128]{1,0:T(8,128)S(1)}, u32[]{:S(2)}, u32[]{:S(2)}) collective-permute-start(f32[56,128]{1,0:T(8,128)S(1)} %shard_map.142.r_0_.r_3_), channel_id=1, source_target_pairs={{0,3},{1,2},{2,1},{3,0},{4,7},{5,6},{6,5},{7,4},{8,11},{9,10},{10,... | collective-permute-start | bytes 86024 | tf_op jit(solution)/shard_map/ppermute | solution.py:80
  17.3 2.2 %collective-permute-start.5 = (f32[40,128]{1,0:T(8,128)S(1)}, f32[40,128]{1,0:T(8,128)S(1)}, u32[]{:S(2)}, u32[]{:S(2)}) collective-permute-start(f32[40,128]{1,0:T(8,128)S(1)} %get-tuple-element.44.r_0_), channel_id=1, source_target_pairs={{0,4},{4,0},{8,12},{12,8},{16,20},{20,16},{24,28},{28,24},{1,5},{5... | collective-permute-start | bytes 61448 | tf_op jit(solution)/shard_map/ppermute | solution.py:73
  17.4 4.2 %collective-permute-start.6 = (f32[40,128]{1,0:T(8,128)S(1)}, f32[40,128]{1,0:T(8,128)S(1)}, u32[]{:S(2)}, u32[]{:S(2)}) collective-permute-start(f32[40,128]{1,0:T(8,128)S(1)} %get-tuple-element.44.r_0_), channel_id=1, source_target_pairs={{0,28},{4,8},{8,4},{12,16},{16,12},{20,24},{24,20},{28,0},{1,29},{... | collective-permute-start | bytes 61448 | tf_op jit(solution)/shard_map/ppermute | solution.py:73
  21.9 6.9 %collective-permute-start.7 = (f32[20,128]{1,0:T(8,128)S(1)}, f32[20,128]{1,0:T(8,128)S(1)}, u32[]{:S(2)}, u32[]{:S(2)}) collective-permute-start(f32[20,128]{1,0:T(8,128)S(1)} %get-tuple-element.51), channel_id=1, source_target_pairs={{0,1},{1,0},{2,3},{3,2},{4,5},{5,4},{6,7},{7,6},{8,9},{9,8},{10,11... | collective-permute-start | bytes 30728 | tf_op jit(solution)/shard_map/ppermute | solution.py:80
  22.0 6.8 %collective-permute-start.8 = (f32[20,128]{1,0:T(8,128)S(1)}, f32[20,128]{1,0:T(8,128)S(1)}, u32[]{:S(2)}, u32[]{:S(2)}) collective-permute-start(f32[20,128]{1,0:T(8,128)S(1)} %get-tuple-element.52), channel_id=1, source_target_pairs={{0,2},{1,3},{2,0},{3,1},{4,6},{5,7},{6,4},{7,5},{8,10},{9,11},{10,... | collective-permute-start | bytes 30728 | tf_op jit(solution)/shard_map/ppermute | solution.py:80
  22.8 6.0 %collective-permute-start.9 = (f32[20,128]{1,0:T(8,128)S(1)}, f32[20,128]{1,0:T(8,128)S(1)}, u32[]{:S(2)}, u32[]{:S(2)}) collective-permute-start(f32[20,128]{1,0:T(8,128)S(1)} %get-tuple-element.53), channel_id=1, source_target_pairs={{0,3},{1,2},{2,1},{3,0},{4,7},{5,6},{6,5},{7,4},{8,11},{9,10},{10,... | collective-permute-start | bytes 30728 | tf_op jit(solution)/shard_map/ppermute | solution.py:80
  29.2 1.2 %collective-permute-start.10 = (f32[8,128]{1,0:T(8,128)S(1)}, f32[8,128]{1,0:T(8,128)S(1)}, u32[]{:S(2)}, u32[]{:S(2)}) collective-permute-start(f32[8,128]{1,0:T(8,128)S(1)} %get-tuple-element.57.own_ref), channel_id=1, source_target_pairs={{0,4},{4,0},{8,12},{12,8},{16,20},{20,16},{24,28},{28,24},{1,5},{5... | collective-permute-start | bytes 12296 | tf_op jit(solution)/shard_map/ppermute | solution.py:73
  29.3 4.0 %collective-permute-start.11 = (f32[8,128]{1,0:T(8,128)S(1)}, f32[8,128]{1,0:T(8,128)S(1)}, u32[]{:S(2)}, u32[]{:S(2)}) collective-permute-start(f32[8,128]{1,0:T(8,128)S(1)} %get-tuple-element.57.own_ref), channel_id=1, source_target_pairs={{0,28},{4,8},{8,4},{12,16},{16,12},{20,24},{24,20},{28,0},{1,29},{... | collective-permute-start | bytes 12296 | tf_op jit(solution)/shard_map/ppermute | solution.py:73
  33.3 4.4 %collective-permute-start.12 = (f32[24,128]{1,0:T(8,128)S(1)}, f32[24,128]{1,0:T(8,128)S(1)}, u32[]{:S(2)}, u32[]{:S(2)}) collective-permute-start(f32[24,128]{1,0:T(8,128)S(1)} %shard_map.149.r_0_), channel_id=1, source_target_pairs={{0,1},{1,0},{2,3},{3,2},{4,5},{5,4},{6,7},{7,6},{8,9},{9,8},{10,11... | collective-permute-start | bytes 36872 | tf_op jit(solution)/shard_map/ppermute | solution.py:80
  33.3 5.3 %collective-permute-start.13 = (f32[24,128]{1,0:T(8,128)S(1)}, f32[24,128]{1,0:T(8,128)S(1)}, u32[]{:S(2)}, u32[]{:S(2)}) collective-permute-start(f32[24,128]{1,0:T(8,128)S(1)} %shard_map.149.r_0_), channel_id=1, source_target_pairs={{0,2},{1,3},{2,0},{3,1},{4,6},{5,7},{6,4},{7,5},{8,10},{9,11},{10,... | collective-permute-start | bytes 36872 | tf_op jit(solution)/shard_map/ppermute | solution.py:80
  36.9 5.5 %collective-permute-start.14 = (f32[24,128]{1,0:T(8,128)S(1)}, f32[24,128]{1,0:T(8,128)S(1)}, u32[]{:S(2)}, u32[]{:S(2)}) collective-permute-start(f32[24,128]{1,0:T(8,128)S(1)} %shard_map.149.r_0_), channel_id=1, source_target_pairs={{0,3},{1,2},{2,1},{3,0},{4,7},{5,6},{6,5},{7,4},{8,11},{9,10},{10,... | collective-permute-start | bytes 36872 | tf_op jit(solution)/shard_map/ppermute | solution.py:80
  42.9 1.3 %collective-permute-start.15 = (f32[40,128]{1,0:T(8,128)S(1)}, f32[40,128]{1,0:T(8,128)S(1)}, u32[]{:S(2)}, u32[]{:S(2)}) collective-permute-start(f32[40,128]{1,0:T(8,128)S(1)} %get-tuple-element.60.r_0_), channel_id=1, source_target_pairs={{0,4},{4,0},{8,12},{12,8},{16,20},{20,16},{24,28},{28,24},{1,5},{5... | collective-permute-start | bytes 61448 | tf_op jit(solution)/shard_map/ppermute | solution.py:73
  43.0 4.2 %collective-permute-start.16 = (f32[40,128]{1,0:T(8,128)S(1)}, f32[40,128]{1,0:T(8,128)S(1)}, u32[]{:S(2)}, u32[]{:S(2)}) collective-permute-start(f32[40,128]{1,0:T(8,128)S(1)} %get-tuple-element.60.r_0_), channel_id=1, source_target_pairs={{0,28},{4,8},{8,4},{12,16},{16,12},{20,24},{24,20},{28,0},{1,29},{... | collective-permute-start | bytes 61448 | tf_op jit(solution)/shard_map/ppermute | solution.py:73
  47.5 6.0 %collective-permute-start.17 = (f32[20,128]{1,0:T(8,128)S(1)}, f32[20,128]{1,0:T(8,128)S(1)}, u32[]{:S(2)}, u32[]{:S(2)}) collective-permute-start(f32[20,128]{1,0:T(8,128)S(1)} %get-tuple-element.67), channel_id=1, source_target_pairs={{0,1},{1,0},{2,3},{3,2},{4,5},{5,4},{6,7},{7,6},{8,9},{9,8},{10,11... | collective-permute-start | bytes 30728 | tf_op jit(solution)/shard_map/ppermute | solution.py:80
  47.6 5.9 %collective-permute-start.18 = (f32[20,128]{1,0:T(8,128)S(1)}, f32[20,128]{1,0:T(8,128)S(1)}, u32[]{:S(2)}, u32[]{:S(2)}) collective-permute-start(f32[20,128]{1,0:T(8,128)S(1)} %get-tuple-element.68), channel_id=1, source_target_pairs={{0,2},{1,3},{2,0},{3,1},{4,6},{5,7},{6,4},{7,5},{8,10},{9,11},{10,... | collective-permute-start | bytes 30728 | tf_op jit(solution)/shard_map/ppermute | solution.py:80
  48.9 5.5 %collective-permute-start.19 = (f32[20,128]{1,0:T(8,128)S(1)}, f32[20,128]{1,0:T(8,128)S(1)}, u32[]{:S(2)}, u32[]{:S(2)}) collective-permute-start(f32[20,128]{1,0:T(8,128)S(1)} %get-tuple-element.69), channel_id=1, source_target_pairs={{0,3},{1,2},{2,1},{3,0},{4,7},{5,6},{6,5},{7,4},{8,11},{9,10},{10,... | collective-permute-start | bytes 30728 | tf_op jit(solution)/shard_map/ppermute | solution.py:80

commit v2 on v1

--- a/solution.py
+++ b/solution.py
@@ -65,6 +65,24 @@
         return owner ^ col
     rest = col - owner
     return jnp.where(rest < 0, rest + n, rest)
+
+
+def slot_section(slot, sec, n):
+    if slot == 0:
+        return sec
+    if n % 2 == 0:
+        step = jnp.where((sec & 1) == (slot & 1), -1, 1)
+    else:
+        step = -1 if slot == 1 else 1
+    at = sec + step
+    return jnp.where(at < 0, at + n, jnp.where(at >= n, at - n, at))
+
+
+def slot_row(j, col, n):
+    if n & (n - 1) == 0:
+        return col ^ j
+    at = col - j
+    return jnp.where(at < 0, at + n, at)
 
 
 def sec_exchange(x):
@@ -280,39 +298,27 @@
     return jnp.take_along_axis(jnp.broadcast_to(row, lane.shape), lane, axis=1)
 
 
-def flux_kernel(later, pieces, cell_rows, *refs):
-    tables, refs = refs[:pieces], refs[pieces:]
-    code_ref, fixed_ref, refs = refs[0], refs[1], refs[2:]
-    if later:
-        top_ref, before_ref, refs = refs[0], refs[1], refs[2:]
-    flux_ref, add_ref = refs
-    ks = code_ref.shape[0]
-    his, lanes, vals = [], [], []
-    for k in range(ks):
-        hi, lane = split(code_ref[k], LANES)
-        his.append(hi)
-        lanes.append(lane)
-        vals.append([jnp.zeros(lane.shape, jnp.float32) for _ in range(2)])
-    for k in range(ks):
+def look_up(codes, cell_rows, pieces, row):
+    found = []
+    for code in codes:
+        hi, lane = split(code, LANES)
+        vals = [jnp.zeros(lane.shape, jnp.float32) for _ in range(2)]
         for slot in range(3):
             for j in range(pieces):
                 for r in range(cell_rows):
-                    hit = his[k] == (slot * pieces + j) * cell_rows + r
-                    base = slot * 2 * cell_rows + r
+                    hit = hi == (slot * pieces + j) * cell_rows + r
                     for v in range(2):
-                        at = base + v * cell_rows
-                        found = lane_gather(tables[j][at : at + 1, :], lanes[k])
-                        vals[k][v] = jnp.where(hit, found, vals[k][v])
-    skin = fixed_ref[ks + 3]
+                        vals[v] = jnp.where(hit, lane_gather(row(slot, j, v * cell_rows + r), lane), vals[v])
+        found.append(vals)
+    return found
+
+
+def surface_fluxes(found, weights, forcing, bottom):
+    short, long_, rain, skin = forcing
     frozen = jnp.zeros_like(skin)
-    for k in range(ks):
-        skin = skin + fixed_ref[k] * vals[k][0]
-        frozen = frozen + fixed_ref[k] * vals[k][1]
-    bottom = [fixed_ref[ks + 4 + f] for f in range(4)]
-    if later:
-        g = top_ref[4]
-        bottom = [top_ref[f] + g * before_ref[f] for f in range(4)]
-    short, long_, rain = fixed_ref[ks], fixed_ref[ks + 1], fixed_ref[ks + 2]
+    for w, vals in zip(weights, found):
+        skin = skin + w * vals[0]
+        frozen = frozen + w * vals[1]
     cover = 1.0 / (1.0 + frozen)
     speed = jnp.sqrt(bottom[2] * bottom[2] + bottom[3] * bottom[3] + 1.0)
     coefficient = 0.3 * speed * cover
@@ -325,11 +331,60 @@
     f5 = long_ - 0.2 * skin
     f6 = rain * (1.0 - snow)
     f7 = rain * snow
-    n = skin.shape[0]
-    for v, value in enumerate((f2, f3, f4 + f5 - f0 - f1, 0.4 * f1 - f6, f7)):
-        flux_ref[v * n : (v + 1) * n] = value
-    for v, value in enumerate((f0, f1, -f2, -f3)):
-        add_ref[v] = value
+    return (f2, f3, f4 + f5 - f0 - f1, 0.4 * f1 - f6, f7), (f0, f1, -f2, -f3)
+
+
+def put_rows(ref, values):
+    n = values[0].shape[0]
+    for v, value in enumerate(values):
+        ref[v * n : (v + 1) * n] = value
+
+
+def first_fluxes(pieces, cell_rows, *refs):
+    tables, (code_ref, fixed_ref, top_ref, flux_ref, add_ref, pack_ref) = refs[:pieces], refs[pieces:]
+    ks = code_ref.shape[0]
+    found = look_up([code_ref[k] for k in range(ks)], cell_rows, pieces,
+                    lambda slot, j, at: tables[j][slot * 2 * cell_rows + at : slot * 2 * cell_rows + at + 1, :])
+    rows = [fixed_ref[i] for i in range(ks + 8)]
+    flux, adds = surface_fluxes(found, rows[:ks], rows[ks : ks + 4], rows[ks + 4 :])
+    put_rows(flux_ref, flux)
+    for f, add in enumerate(adds):
+        add_ref[f] = add
+        pack_ref[f] = top_ref[f] + top_ref[4] * add
+    for k in range(ks):
+        pack_ref[4 + k] = code_ref[k].astype(jnp.float32)
+    for i in range(ks + 4):
+        pack_ref[4 + ks + i] = rows[i]
+
+
+def packed_fluxes(pack_ref, cell_rows, pieces, row, flux_ref, add_ref):
+    ks = (pack_ref.shape[0] - 8) // 2
+    found = look_up([pack_ref[4 + k].astype(jnp.int32) for k in range(ks)], cell_rows, pieces, row)
+    rows = [pack_ref[4 + ks + i] for i in range(ks + 4)]
+    flux, adds = surface_fluxes(found, rows[:ks], rows[ks:], [pack_ref[f] for f in range(4)])
+    put_rows(flux_ref, flux)
+    if add_ref is not None:
+        for f, add in enumerate(adds):
+            add_ref[f] = add
+
+
+def later_fluxes(pieces, cell_rows, *refs):
+    tables, (pack_ref, flux_ref, add_ref) = refs[:pieces], refs[pieces:]
+    packed_fluxes(pack_ref, cell_rows, pieces,
+                  lambda slot, j, at: tables[j][slot * 2 * cell_rows + at : slot * 2 * cell_rows + at + 1, :],
+                  flux_ref, add_ref)
+
+
+def wide_fluxes(secs, cols, cell_rows, all_ref, *refs):
+    packs, fluxes, add_ref = refs[:3], refs[3:6], refs[6]
+    sec, col = lax.axis_index("sec"), lax.axis_index("col")
+    for n in range(3):
+        home = slot_section(n, sec, secs)
+        owners = [slot_section(slot, home, secs) * cols for slot in range(3)]
+        places = [slot_row(j, col, cols) for j in range(cols)]
+        packed_fluxes(packs[n], cell_rows, cols,
+                      lambda slot, j, at: all_ref[owners[slot] + places[j], at : at + 1, :],
+                      fluxes[n], None if n else add_ref)
 
 
 def partial_kernel(offset, slots, pieces, *refs):
@@ -370,11 +425,13 @@
             outs[j][at] = whole + before[j][at] if before else whole
 
 
-def sea_kernel(pieces, depth, last, *refs):
+def sea_kernel(pieces, depth, last, spread, *refs):
     parts, refs = refs[:pieces], refs[pieces:]
     state_ref, mix_ref, ice_ref, mask_ref, refs = refs[0], refs[1], refs[2], refs[3], refs[4:]
     if last:
         out_hbm, top_hbm, fac, work, out_ref, top_ref, sems = refs
+    elif spread:
+        out_ref, top_ref, all_ref, fac, work = refs
     else:
         out_ref, top_ref, fac, work = refs
     tiles = mix_ref.shape[0] // depth
@@ -438,6 +495,9 @@
             copies[-1].start()
     for c in copies:
         c.wait()
+    if spread:
+        for i in range(all_ref.shape[0]):
+            all_ref[i] = top_ref[...]
 
 
 def air_finish(y2_ref, hg_ref, first_ref, second_ref, out_ref):
@@ -507,38 +567,59 @@
                  pltpu.SemaphoreType.DMA((fields + 3,))],
     )
     bundles = col_exchange([bundle] * cols)
+    wide = cols * secs <= 64
     adds, tables = [], bundles
+    flux_out = ((FLUXES * tiles, LANES), f32)
+    add_out = ((fields, tiles, LANES), f32)
+    share = ((FLUXES * sea_tiles, LANES), f32)
+
+    def sums(slots, peers, *args):
+        return call(lambda *r: partial_kernel(offset, slots, len(peers), *r), [share] * len(peers), *args)
+
     for step in range(STEPS):
-        extra = (tops, adds[0]) if step else ()
-        flux, add = call(
-            lambda *r: flux_kernel(bool(step), cols, sea_tiles, *r),
-            [((FLUXES * tiles, LANES), f32), ((fields, tiles, LANES), f32)],
-            *tables, code, fixed, *extra,
-        )
+        last = step == STEPS - 1
+        peers = bundles[1:]
+        if step and wide:
+            flux, *near, add = call(
+                lambda *r: wide_fluxes(secs, cols, sea_tiles, *r), [flux_out] * 3 + [add_out], everywhere, pack, *halo
+            )
+            parts = sums((0, 1, 2), peers, flux, *near, *peers)
+        else:
+            if step:
+                flux, add = call(lambda *r: later_fluxes(cols, sea_tiles, *r), [flux_out, add_out], *tables, pack)
+            else:
+                flux, add, pack = call(
+                    lambda *r: first_fluxes(cols, sea_tiles, *r),
+                    [flux_out, add_out, ((2 * ko + 8, tiles, LANES), f32)], *tables, code, fixed, tops,
+                )
+            near = sec_exchange(flux)
+            parts = sums((0,), peers, flux, *peers)
+            parts = sums((1,), peers, near[0], *peers, *parts)
+            parts = sums((2,), peers, near[1], *peers, *parts)
         adds.append(add)
-        near = sec_exchange(flux)
-        share = ((FLUXES * sea_tiles, LANES), f32)
-        sums = lambda slots, peers, *args: call(
-            lambda *r: partial_kernel(offset, slots, len(peers), *r), [share] * len(peers), *args)
-        parts = sums((0,), bundles[1:], flux, *bundles[1:])
-        parts = sums((1,), bundles[1:], near[0], *bundles[1:], *parts)
-        parts = sums((2,), bundles[1:], near[1], *bundles[1:], *parts)
         moved = col_exchange([flux, *parts])
         moved[:1] = sums((0, 1, 2), bundles[:1], flux, *near, bundles[0])
-        last = step == STEPS - 1
         if last:
             (air_out,) = call(air_finish, [(air.shape, f32)], y2, hg, *adds, out_space=None)
-        solve_scratch = [pltpu.VMEM((3, depth, sea_tiles, LANES), f32), pltpu.VMEM((2, depth, sea_tiles, LANES), f32)]
-        sea, top = call(
-            lambda *r: sea_kernel(cols, depth, last, *r),
-            [(sea.shape, f32), ((sea_tiles if last else 2 * sea_tiles, LANES), f32)],
+        elif wide:
+            halo = sec_exchange(pack)
+        spread = wide and not last
+        sea, top, *rest = call(
+            lambda *r: sea_kernel(cols, depth, last, spread, *r),
+            [(sea.shape, f32), ((sea_tiles if last else 2 * sea_tiles, LANES), f32)]
+            + [((secs * cols, 2 * sea_tiles, LANES), f32)] * spread,
             *moved, sea, sea_k, ice, wet, out_space=hbm if last else pltpu.VMEM,
-            scratch=solve_scratch + ([vmem(sea), vmem(ice), pltpu.SemaphoreType.DMA((3,))] if last else []),
+            scratch=[pltpu.VMEM((3, depth, sea_tiles, LANES), f32), pltpu.VMEM((2, depth, sea_tiles, LANES), f32)]
+            + ([vmem(sea), vmem(ice), pltpu.SemaphoreType.DMA((3,))] if last else []),
         )
         if not last:
             ice = top[sea_tiles:]
-            (bundle,) = call(later_bundle, [((offset, LANES), f32)], top, *sec_exchange(top))
-            tables = col_exchange([bundle] * cols)
+            if wide:
+                ready, *halo = lax.optimization_barrier((rest[0], *halo))
+                everywhere = lax.all_to_all(ready, ("sec", "col"), 0, 0)
+            else:
+                (bundle,) = call(later_bundle, [((offset, LANES), f32)], top, *sec_exchange(top))
+                tables = col_exchange([bundle] * cols)
     return (untile_rows(air_out, levels, here), untile_rows(sea, depth, cells), top.reshape(cells))
 
 

time: 55.8 us -> 53.8 us (0.964)
  blocking collectives: 0 us -> 11.9 us
  waiting for transfers between devices: 19.1 us -> 9.07 us
  starting transfers between devices: 25.2 us -> 20.6 us
  Pallas kernels: 10.4 us -> 11.1 us
    all_to_all x0 -> x1, blocking collectives: none -> 11.9 us  [per_device(): everywhere = lax.all_to_all(ready, ('sec', 'col'), 0, 0)]
    ppermute x8 -> x6, waiting for transfers between devices: 7.93 us -> 2.17 us  [sec_exchange(): got.append(lax.ppermute(x, 'sec', pairs))]
    ppermute x12 -> x9, starting transfers between devices: 17.7 us -> 13.3 us  [col_exchange(): got.append(lax.ppermute(pieces[j], 'col', col_pairs(j)))]
    ppermute x12 -> x9, waiting for transfers between devices: 11.2 us -> 6.9 us  [col_exchange(): got.append(lax.ppermute(pieces[j], 'col', col_pairs(j)))]
    pallas_call x18 -> x15, Pallas kernels: 10.4 us -> 11.1 us  [call(): pl.pallas_call(kernel, out_shape=[pltpu.VMEM(*o) if sp is pltpu.VMEM else...]
    ppermute x8 -> x6, starting transfers between devices: 7.51 us -> 7.37 us  [sec_exchange(): got.append(lax.ppermute(x, 'sec', pairs))]
  transfers between devices with their start and end apart: 20 -> 15, of which waited for: 11 -> 6; matrix products, arithmetic and copies ran while one was open for 0% -> 0% of each run, Pallas kernels for 12% -> 12%
where the time goes in v2:
time: 53.8 us; the launch traced here: 53.5 us
  starting transfers between devices  20.6 us (38%)
  blocking collectives  11.9 us (22%)
  Pallas kernels  11.1 us (21%)
  waiting for transfers between devices  9.07 us (17%)
  between operations  0.81 us (2%)
    ppermute x9, starting transfers between devices, col_exchange(): got.append(lax.ppermute(pieces[j], 'col', col_pairs(j)))  13.3 us
    all_to_all x1, blocking collectives, per_device(): everywhere = lax.all_to_all(ready, ('sec', 'col'), 0, 0)  11.9 us
    pallas_call x15, Pallas kernels, call(): pl.pallas_call(kernel, out_shape=[pltpu.VMEM(*o) if sp is pltpu.VMEM else...  11.1 us
    ppermute x6, starting transfers between devices, sec_exchange(): got.append(lax.ppermute(x, 'sec', pairs))  7.37 us
    ppermute x9, waiting for transfers between devices, col_exchange(): got.append(lax.ppermute(pieces[j], 'col', col_pairs(j)))  6.9 us
    ppermute x6, waiting for transfers between devices, sec_exchange(): got.append(lax.ppermute(x, 'sec', pairs))  2.17 us
  transfers between devices with their start and end apart: 15, of which 6 were waited for; matrix products, arithmetic and copies ran while one was open for 0% of the time, Pallas kernels for 12%

profile of v2, /device:TPU:0, one launch (start us, length us, event | category | flops | bytes accessed | tf_op | source)
XLA Modules:
  0.0 53.5 jit_solution(16939417830640819463)
XLA Ops:
  0.6 0.7 %shard_map.140.own_ref = f32[8,128]{1,0:T(8,128)S(1)} custom-call(f32[2,320,128]{2,1,0:T(8,128)} %bitcast.61, f32[4,128]{1,0:T(4,128)} %bitcast.72), custom_call_target="tpu_custom_call" | custom-call | tf_op jit(solution)/shard_map/pallas_call | solution.py:517
  1.4 0.6 %collective-permute-start = (f32[8,128]{1,0:T(8,128)S(1)}, f32[8,128]{1,0:T(8,128)S(1)}, u32[]{:S(2)}, u32[]{:S(2)}) collective-permute-start(f32[8,128]{1,0:T(8,128)S(1)} %shard_map.140.own_ref), channel_id=1, source_target_pairs={{0,4},{4,0},{8,12},{12,8},{16,20},{20,16},{24,28},{28,24},{1,5},{5... | collective-permute-start | bytes 12296 | tf_op jit(solution)/shard_map/ppermute | solution.py:91
  1.9 3.5 %collective-permute-start.1 = (f32[8,128]{1,0:T(8,128)S(1)}, f32[8,128]{1,0:T(8,128)S(1)}, u32[]{:S(2)}, u32[]{:S(2)}) collective-permute-start(f32[8,128]{1,0:T(8,128)S(1)} %shard_map.140.own_ref), channel_id=1, source_target_pairs={{0,28},{4,8},{8,4},{12,16},{16,12},{20,24},{24,20},{28,0},{1,29},{... | collective-permute-start | bytes 12296 | tf_op jit(solution)/shard_map/ppermute | solution.py:91
  5.5 1.1 %shard_map.141 = (s32[4,8,128]{2,1,0:T(8,128)S(1)}, f32[12,8,128]{2,1,0:T(8,128)S(1)}, f32[32,128]{1,0:T(8,128)S(1)}, s32[4,128]{1,0:T(4,128)S(1)}) custom-call(f32[4,512,128]{2,1,0:T(8,128)} %bitcast.59, s32[32,128]{1,0:T(8,128)} %bitcast.66, f32[32,128]{1,0:T(8,128)} %bitcast.67, f32[32,128]{1,0:T(8,128)} %bitcast.68, s32[8,128]{1,0:T(8,128)} %bitcast.71, ...), custom_call_target="tpu_custom_call" | custom-call | tf_op jit(solution)/shard_map/pallas_call | solution.py:517
  6.8 1.7 %collective-permute-start.2 = (f32[56,128]{1,0:T(8,128)S(1)}, f32[56,128]{1,0:T(8,128)S(1)}, u32[]{:S(2)}, u32[]{:S(2)}) collective-permute-start(f32[56,128]{1,0:T(8,128)S(1)} %shard_map.142.r_0_.r_3_), channel_id=1, source_target_pairs={{0,1},{1,0},{2,3},{3,2},{4,5},{5,4},{6,7},{7,6},{8,9},{9,8},{10,11... | collective-permute-start | bytes 86024 | tf_op jit(solution)/shard_map/ppermute | solution.py:98
  8.5 2.6 %collective-permute-start.3 = (f32[56,128]{1,0:T(8,128)S(1)}, f32[56,128]{1,0:T(8,128)S(1)}, u32[]{:S(2)}, u32[]{:S(2)}) collective-permute-start(f32[56,128]{1,0:T(8,128)S(1)} %shard_map.142.r_0_.r_3_), channel_id=1, source_target_pairs={{0,2},{1,3},{2,0},{3,1},{4,6},{5,7},{6,4},{7,5},{8,10},{9,11},{10,... | collective-permute-start | bytes 86024 | tf_op jit(solution)/shard_map/ppermute | solution.py:98
  11.2 2.1 %shard_map.139 = (f32[4,512,128]{2,1,0:T(8,128)S(1)}, f32[2,512,128]{2,1,0:T(8,128)S(1)}, f32[5,8,128]{2,1,0:T(8,128)S(1)}, f32[2,320,128]{2,1,0:T(8,128)S(1)}, f32[320,128]{1,0:T(8,128)S(1)}) custom-call(f32[4,512,128]{2,1,0:T(8,128)} %bitcast.60, f32[512,128]{1,0:T(8,128)} %bitcast.64, f32[2,320,128]{2,1,0:T(8,128)} %bitcast.62, f32[320,128]{1,0:T(8,128)} %bitcast.65), custom_call_target="tpu_custom_call" | custom-call | tf_op jit(solution)/shard_map/pallas_call | solution.py:517
  13.3 0.5 collective-permute-done.3.r_2_.r_4_
  13.8 3.0 %collective-permute-done.4.r_3_.r_5_ = f32[56,128]{1,0:T(8,128)S(1)} collective-permute-done((f32[56,128]{1,0:T(8,128)S(1)}, f32[56,128]{1,0:T(8,128)S(1)}, u32[]{:S(2)}, u32[]{:S(2)}) %collective-permute-start.4) | collective-permute-done | bytes 28704 | tf_op jit(solution)/shard_map/ppermute | solution.py:98
  16.8 0.5 shard_map.143
  17.4 1.8 %collective-permute-start.11 = (f32[16,8,128]{2,1,0:T(8,128)S(1)}, f32[16,8,128]{2,1,0:T(8,128)S(1)}, u32[]{:S(2)}, u32[]{:S(2)}) collective-permute-start(f32[16,8,128]{2,1,0:T(8,128)S(1)} %get-tuple-element.60.r_1_), channel_id=1, source_target_pairs={{0,28},{4,8},{8,4},{12,16},{16,12},{20,24},{24,20},{28,0},{1,29},{... | collective-permute-start | bytes 196616 | tf_op jit(solution)/shard_map/ppermute | solution.py:91
  19.1 1.4 %collective-permute-start.6 = (f32[40,128]{1,0:T(8,128)S(1)}, f32[40,128]{1,0:T(8,128)S(1)}, u32[]{:S(2)}, u32[]{:S(2)}) collective-permute-start(f32[40,128]{1,0:T(8,128)S(1)} %get-tuple-element.46.r_0_), channel_id=1, source_target_pairs={{0,28},{4,8},{8,4},{12,16},{16,12},{20,24},{24,20},{28,0},{1,29},{... | collective-permute-start | bytes 61448 | tf_op jit(solution)/shard_map/ppermute | solution.py:91
  21.3 2.0 %collective-permute-done.6.r_2_.r_0_ = f32[40,128]{1,0:T(8,128)S(1)} collective-permute-done((f32[40,128]{1,0:T(8,128)S(1)}, f32[40,128]{1,0:T(8,128)S(1)}, u32[]{:S(2)}, u32[]{:S(2)}) %collective-permute-start.6) | collective-permute-done | bytes 20512 | tf_op jit(solution)/shard_map/ppermute | solution.py:91
  23.7 1.4 %collective-permute-start.8 = (f32[20,128]{1,0:T(8,128)S(1)}, f32[20,128]{1,0:T(8,128)S(1)}, u32[]{:S(2)}, u32[]{:S(2)}) collective-permute-start(f32[20,128]{1,0:T(8,128)S(1)} %get-tuple-element.54), channel_id=1, source_target_pairs={{0,2},{1,3},{2,0},{3,1},{4,6},{5,7},{6,4},{7,5},{8,10},{9,11},{10,... | collective-permute-start | bytes 30728 | tf_op jit(solution)/shard_map/ppermute | solution.py:98
  25.0 3.0 %collective-permute-start.9 = (f32[20,128]{1,0:T(8,128)S(1)}, f32[20,128]{1,0:T(8,128)S(1)}, u32[]{:S(2)}, u32[]{:S(2)}) collective-permute-start(f32[20,128]{1,0:T(8,128)S(1)} %get-tuple-element.55), channel_id=1, source_target_pairs={{0,3},{1,2},{2,1},{3,0},{4,7},{5,6},{6,5},{7,4},{8,11},{9,10},{10,... | collective-permute-start | bytes 30728 | tf_op jit(solution)/shard_map/ppermute | solution.py:98
  28.4 2.1 %collective-permute-done.9.r_3_ = f32[20,128]{1,0:T(8,128)S(1)} collective-permute-done((f32[20,128]{1,0:T(8,128)S(1)}, f32[20,128]{1,0:T(8,128)S(1)}, u32[]{:S(2)}, u32[]{:S(2)}) %collective-permute-start.9) | collective-permute-done | bytes 10272 | tf_op jit(solution)/shard_map/ppermute | solution.py:98
  31.0 11.9 %all_to_all.5.r_0_ = f32[32,8,128]{2,1,0:T(8,128)S(1)} all-to-all(f32[32,8,128]{2,1,0:T(8,128)S(1)} %get-tuple-element.61), channel_id=1, replica_groups=mesh['sec'=8,'col'=4] {'sec','col'}, dimensions={0} | all-to-all | bytes 262144 | tf_op jit(solution)/shard_map/all_to_all | solution.py:619
  42.8 1.4 %shard_map.149 = (f32[40,128]{1,0:T(8,128)S(1)}, f32[40,128]{1,0:T(8,128)S(1)}, f32[40,128]{1,0:T(8,128)S(1)}, f32[4,8,128]{2,1,0:T(8,128)S(1)}) custom-call(f32[32,8,128]{2,1,0:T(8,128)S(1)} %all_to_all.5.r_0_, f32[16,8,128]{2,1,0:T(8,128)S(1)} %get-tuple-element.60.r_1_, f32[16,8,128]{2,1,0:T(8,128)S(1)} %collective-permute-done.10.r_2_, ...), custom_call_target="tpu_custom_call" | custom-call | tf_op jit(solution)/shard_map/pallas_call | solution.py:517
  44.2 0.9 %shard_map.152 = (f32[20,128]{1,0:T(8,128)S(1)}, f32[20,128]{1,0:T(8,128)S(1)}, f32[20,128]{1,0:T(8,128)S(1)}) custom-call(f32[40,128]{1,0:T(8,128)S(1)} %get-tuple-element.65.r_0_, f32[40,128]{1,0:T(8,128)S(1)} %get-tuple-element.66.r_1_, f32[40,128]{1,0:T(8,128)S(1)} %get-tuple-element.67.r_2_, f32[56,128]{1,0:T(8,128)S(1)} %collective-permute-done.2.r_1_.r_3_, ...), custom_call_target="tpu_custom_call" | custom-call | tf_op jit(solution)/shard_map/pallas_call | solution.py:517
  45.2 1.7 %collective-permute-start.13 = (f32[20,128]{1,0:T(8,128)S(1)}, f32[20,128]{1,0:T(8,128)S(1)}, u32[]{:S(2)}, u32[]{:S(2)}) collective-permute-start(f32[20,128]{1,0:T(8,128)S(1)} %get-tuple-element.69), channel_id=1, source_target_pairs={{0,2},{1,3},{2,0},{3,1},{4,6},{5,7},{6,4},{7,5},{8,10},{9,11},{10,... | collective-permute-start | bytes 30728 | tf_op jit(solution)/shard_map/ppermute | solution.py:98
  46.9 2.6 %collective-permute-start.14 = (f32[20,128]{1,0:T(8,128)S(1)}, f32[20,128]{1,0:T(8,128)S(1)}, u32[]{:S(2)}, u32[]{:S(2)}) collective-permute-start(f32[20,128]{1,0:T(8,128)S(1)} %get-tuple-element.70), channel_id=1, source_target_pairs={{0,3},{1,2},{2,1},{3,0},{4,7},{5,6},{6,5},{7,4},{8,11},{9,10},{10,... | collective-permute-start | bytes 30728 | tf_op jit(solution)/shard_map/ppermute | solution.py:98
  49.9 1.2 %shard_map.150 = f32[4,512,128]{2,1,0:T(8,128)} custom-call(f32[4,512,128]{2,1,0:T(8,128)S(1)} %get-tuple-element.39.y2_ref, f32[2,512,128]{2,1,0:T(8,128)S(1)} %get-tuple-element.40.hg_ref, f32[4,8,128]{2,1,0:T(8,128)S(1)} %get-tuple-element.45.first_ref, f32[4,8,128]{2,1,0:T(8,128)S(1)} %get-tuple-element.64.second_ref), custom_call_target="tpu_custom_call" | custom-call | tf_op jit(solution)/shard_map/pallas_call | solution.py:517
  51.1 1.3 %collective-permute-done.14.r_3_ = f32[20,128]{1,0:T(8,128)S(1)} collective-permute-done((f32[20,128]{1,0:T(8,128)S(1)}, f32[20,128]{1,0:T(8,128)S(1)}, u32[]{:S(2)}, u32[]{:S(2)}) %collective-permute-start.14) | collective-permute-done | bytes 10272 | tf_op jit(solution)/shard_map/ppermute | solution.py:98
  52.4 1.1 %shard_map.153 = (f32[2,320,128]{2,1,0:T(8,128)}, f32[4,128]{1,0:T(4,128)}) custom-call(f32[20,128]{1,0:T(8,128)S(1)} %shard_map.151.r_0_, f32[20,128]{1,0:T(8,128)S(1)} %collective-permute-done.12.r_1_, f32[20,128]{1,0:T(8,128)S(1)} %collective-permute-done.13.r_2_, f32[20,128]{1,0:T(8,128)S(1)} %collective-permute-done.14.r_3_, ...), custom_call_target="tpu_custom_call" | custom-call | tf_op jit(solution)/shard_map/pallas_call | solution.py:517
  (24 shorter events, 2.7 us)
Async XLA Ops:
  1.4 5.2 %collective-permute-start = (f32[8,128]{1,0:T(8,128)S(1)}, f32[8,128]{1,0:T(8,128)S(1)}, u32[]{:S(2)}, u32[]{:S(2)}) collective-permute-start(f32[8,128]{1,0:T(8,128)S(1)} %shard_map.140.own_ref), channel_id=1, source_target_pairs={{0,4},{4,0},{8,12},{12,8},{16,20},{20,16},{24,28},{28,24},{1,5},{5... | collective-permute-start | bytes 12296 | tf_op jit(solution)/shard_map/ppermute | solution.py:91
  1.9 4.9 %collective-permute-start.1 = (f32[8,128]{1,0:T(8,128)S(1)}, f32[8,128]{1,0:T(8,128)S(1)}, u32[]{:S(2)}, u32[]{:S(2)}) collective-permute-start(f32[8,128]{1,0:T(8,128)S(1)} %shard_map.140.own_ref), channel_id=1, source_target_pairs={{0,28},{4,8},{8,4},{12,16},{16,12},{20,24},{24,20},{28,0},{1,29},{... | collective-permute-start | bytes 12296 | tf_op jit(solution)/shard_map/ppermute | solution.py:91
  6.8 6.5 %collective-permute-start.2 = (f32[56,128]{1,0:T(8,128)S(1)}, f32[56,128]{1,0:T(8,128)S(1)}, u32[]{:S(2)}, u32[]{:S(2)}) collective-permute-start(f32[56,128]{1,0:T(8,128)S(1)} %shard_map.142.r_0_.r_3_), channel_id=1, source_target_pairs={{0,1},{1,0},{2,3},{3,2},{4,5},{5,4},{6,7},{7,6},{8,9},{9,8},{10,11... | collective-permute-start | bytes 86024 | tf_op jit(solution)/shard_map/ppermute | solution.py:98
  8.5 5.2 %collective-permute-start.3 = (f32[56,128]{1,0:T(8,128)S(1)}, f32[56,128]{1,0:T(8,128)S(1)}, u32[]{:S(2)}, u32[]{:S(2)}) collective-permute-start(f32[56,128]{1,0:T(8,128)S(1)} %shard_map.142.r_0_.r_3_), channel_id=1, source_target_pairs={{0,2},{1,3},{2,0},{3,1},{4,6},{5,7},{6,4},{7,5},{8,10},{9,11},{10,... | collective-permute-start | bytes 86024 | tf_op jit(solution)/shard_map/ppermute | solution.py:98
  11.1 5.7 %collective-permute-start.4 = (f32[56,128]{1,0:T(8,128)S(1)}, f32[56,128]{1,0:T(8,128)S(1)}, u32[]{:S(2)}, u32[]{:S(2)}) collective-permute-start(f32[56,128]{1,0:T(8,128)S(1)} %shard_map.142.r_0_.r_3_), channel_id=1, source_target_pairs={{0,3},{1,2},{2,1},{3,0},{4,7},{5,6},{6,5},{7,4},{8,11},{9,10},{10,... | collective-permute-start | bytes 86024 | tf_op jit(solution)/shard_map/ppermute | solution.py:98
  17.3 13.7 %collective-permute-start.10 = (f32[16,8,128]{2,1,0:T(8,128)S(1)}, f32[16,8,128]{2,1,0:T(8,128)S(1)}, u32[]{:S(2)}, u32[]{:S(2)}) collective-permute-start(f32[16,8,128]{2,1,0:T(8,128)S(1)} %get-tuple-element.60.r_1_), channel_id=1, source_target_pairs={{0,4},{4,0},{8,12},{12,8},{16,20},{20,16},{24,28},{28,24},{1,5},{5... | collective-permute-start | bytes 196616 | tf_op jit(solution)/shard_map/ppermute | solution.py:91
  17.4 13.6 %collective-permute-start.11 = (f32[16,8,128]{2,1,0:T(8,128)S(1)}, f32[16,8,128]{2,1,0:T(8,128)S(1)}, u32[]{:S(2)}, u32[]{:S(2)}) collective-permute-start(f32[16,8,128]{2,1,0:T(8,128)S(1)} %get-tuple-element.60.r_1_), channel_id=1, source_target_pairs={{0,28},{4,8},{8,4},{12,16},{16,12},{20,24},{24,20},{28,0},{1,29},{... | collective-permute-start | bytes 196616 | tf_op jit(solution)/shard_map/ppermute | solution.py:91
  19.1 1.8 %collective-permute-start.5 = (f32[40,128]{1,0:T(8,128)S(1)}, f32[40,128]{1,0:T(8,128)S(1)}, u32[]{:S(2)}, u32[]{:S(2)}) collective-permute-start(f32[40,128]{1,0:T(8,128)S(1)} %get-tuple-element.46.r_0_), channel_id=1, source_target_pairs={{0,4},{4,0},{8,12},{12,8},{16,20},{20,16},{24,28},{28,24},{1,5},{5... | collective-permute-start | bytes 61448 | tf_op jit(solution)/shard_map/ppermute | solution.py:91
  19.1 4.1 %collective-permute-start.6 = (f32[40,128]{1,0:T(8,128)S(1)}, f32[40,128]{1,0:T(8,128)S(1)}, u32[]{:S(2)}, u32[]{:S(2)}) collective-permute-start(f32[40,128]{1,0:T(8,128)S(1)} %get-tuple-element.46.r_0_), channel_id=1, source_target_pairs={{0,28},{4,8},{8,4},{12,16},{16,12},{20,24},{24,20},{28,0},{1,29},{... | collective-permute-start | bytes 61448 | tf_op jit(solution)/shard_map/ppermute | solution.py:91
  23.6 4.8 %collective-permute-start.7 = (f32[20,128]{1,0:T(8,128)S(1)}, f32[20,128]{1,0:T(8,128)S(1)}, u32[]{:S(2)}, u32[]{:S(2)}) collective-permute-start(f32[20,128]{1,0:T(8,128)S(1)} %get-tuple-element.53), channel_id=1, source_target_pairs={{0,1},{1,0},{2,3},{3,2},{4,5},{5,4},{6,7},{7,6},{8,9},{9,8},{10,11... | collective-permute-start | bytes 30728 | tf_op jit(solution)/shard_map/ppermute | solution.py:98
  23.7 4.7 %collective-permute-start.8 = (f32[20,128]{1,0:T(8,128)S(1)}, f32[20,128]{1,0:T(8,128)S(1)}, u32[]{:S(2)}, u32[]{:S(2)}) collective-permute-start(f32[20,128]{1,0:T(8,128)S(1)} %get-tuple-element.54), channel_id=1, source_target_pairs={{0,2},{1,3},{2,0},{3,1},{4,6},{5,7},{6,4},{7,5},{8,10},{9,11},{10,... | collective-permute-start | bytes 30728 | tf_op jit(solution)/shard_map/ppermute | solution.py:98
  25.0 5.5 %collective-permute-start.9 = (f32[20,128]{1,0:T(8,128)S(1)}, f32[20,128]{1,0:T(8,128)S(1)}, u32[]{:S(2)}, u32[]{:S(2)}) collective-permute-start(f32[20,128]{1,0:T(8,128)S(1)} %get-tuple-element.55), channel_id=1, source_target_pairs={{0,3},{1,2},{2,1},{3,0},{4,7},{5,6},{6,5},{7,4},{8,11},{9,10},{10,... | collective-permute-start | bytes 30728 | tf_op jit(solution)/shard_map/ppermute | solution.py:98
  45.1 6.0 %collective-permute-start.12 = (f32[20,128]{1,0:T(8,128)S(1)}, f32[20,128]{1,0:T(8,128)S(1)}, u32[]{:S(2)}, u32[]{:S(2)}) collective-permute-start(f32[20,128]{1,0:T(8,128)S(1)} %get-tuple-element.68), channel_id=1, source_target_pairs={{0,1},{1,0},{2,3},{3,2},{4,5},{5,4},{6,7},{7,6},{8,9},{9,8},{10,11... | collective-permute-start | bytes 30728 | tf_op jit(solution)/shard_map/ppermute | solution.py:98
  45.2 5.9 %collective-permute-start.13 = (f32[20,128]{1,0:T(8,128)S(1)}, f32[20,128]{1,0:T(8,128)S(1)}, u32[]{:S(2)}, u32[]{:S(2)}) collective-permute-start(f32[20,128]{1,0:T(8,128)S(1)} %get-tuple-element.69), channel_id=1, source_target_pairs={{0,2},{1,3},{2,0},{3,1},{4,6},{5,7},{6,4},{7,5},{8,10},{9,11},{10,... | collective-permute-start | bytes 30728 | tf_op jit(solution)/shard_map/ppermute | solution.py:98
  46.9 5.5 %collective-permute-start.14 = (f32[20,128]{1,0:T(8,128)S(1)}, f32[20,128]{1,0:T(8,128)S(1)}, u32[]{:S(2)}, u32[]{:S(2)}) collective-permute-start(f32[20,128]{1,0:T(8,128)S(1)} %get-tuple-element.70), channel_id=1, source_target_pairs={{0,3},{1,2},{2,1},{3,0},{4,7},{5,6},{6,5},{7,4},{8,11},{9,10},{10,... | collective-permute-start | bytes 30728 | tf_op jit(solution)/shard_map/ppermute | solution.py:98
